TPU v7x, 32 devices: a whole 2x2x4 slice. The times are simulated.
32 devices in a mesh: sec: 2 (over y), ty: 4 (over x, core), tx: 4 (over z).
Axes of the slice: x: 2, y: 2, z: 4, core: 2. Of those that a mesh axis runs over, the one named last changes fastest.
Arguments:
- images: float32 [2, 1024, 2048], P('sec', 'ty', 'tx'), may hold values from -12 to 12
Outputs:
- relaxed: float32 [2, 2, 16, 32], P('sec', None, 'ty', 'tx')
- cumulative: float32 [2, 2, 16, 32], P('sec', None, 'ty', 'tx')
All inputs are finite; a program needn't handle non-finite values.
Results may differ from a plain program's by a relative error of at most 0.0003.
Values sent between devices are 32-bit elements; how exact they have to be, the bound alone decides.
No kernel may reach another device: no remote copies, remote signals or barrier semaphores. Data moves between devices by JAX's collectives and lax.ppermute only.
A program may use at most 64 MiB of HBM per device.

v0:
```python
import functools

import jax
import jax.numpy as jnp
import numpy as np
from jax import lax
from jax.experimental import pallas as pl
from jax.experimental.pallas import tpu as pltpu
from jax.sharding import PartitionSpec as P


PATCH = 128
STRIDE = 64
HALF = STRIDE // 2
FREQ = -(-(PATCH // 2 + 1) // 8) * 8

stiffness = 1.0
rate = 0.25


def two_parts(table):
    high = table.astype(jnp.bfloat16)
    low = (table - high.astype(np.float64)).astype(jnp.bfloat16)
    return high, low


def tables():
    angle = 2.0 * np.pi * (np.outer(np.arange(PATCH), np.arange(PATCH)) % PATCH) / PATCH
    cosine, sine = np.cos(angle), np.sin(angle)
    kept = np.arange(FREQ)[:, None] <= PATCH // 2
    left = np.concatenate([cosine[:FREQ] * kept, -sine[:FREQ] * kept])
    right = np.block([[cosine, -sine], [sine, cosine]])
    share = np.where((np.arange(FREQ) == 0) | (np.arange(FREQ) == PATCH // 2), 1.0, 2.0)
    scaled = (share * kept[:, 0])[None, :] / float(PATCH) ** 3
    back = np.concatenate([cosine[:, :FREQ] * scaled, sine[:, :FREQ] * scaled], axis=1)
    left_hi, left_lo = two_parts(left)
    back_hi, back_lo = two_parts(back)
    right_hi, right_lo = two_parts(right)
    return (
        np.concatenate([left_hi, left_hi, left_lo], axis=1),
        np.stack([right_hi, right_lo]),
        np.concatenate([back_hi, back_hi, back_lo], axis=1),
    )


def split(values):
    high = values.astype(jnp.bfloat16)
    return high, (values - high.astype(jnp.float32)).astype(jnp.bfloat16)


def mul(a, b):
    return jnp.dot(a, b, preferred_element_type=jnp.float32)


def right_dft(values, right_ref):
    high, low = split(values)
    return mul(high, right_ref[0]) + mul(low, right_ref[0]) + mul(high, right_ref[1])


def node_order(cols):
    return [2 * t for t in range(cols // 2)] + [2 * t + 1 for t in range(cols // 2)]


def keep_region(region, wide, high_ref, low_ref):
    even, odd = region[:, :wide], region[:, STRIDE:STRIDE + wide]
    for part, values in enumerate((even, odd)):
        high, low = split(values)
        high_ref[:, part * wide:(part + 1) * wide] = high
        low_ref[:, part * wide:(part + 1) * wide] = low


def left_dft(cols, bands, high_ref, low_ref, left_ref, half_ref):
    for k, i in enumerate(bands):
        band = pl.ds(i * STRIDE, PATCH)
        high = high_ref[band, :]
        stacked = jnp.concatenate([high, low_ref[band, :], high], axis=0)
        out = mul(left_ref[...], stacked)
        for t, j in enumerate(node_order(cols)):
            lanes = slice(t * PATCH, (t + 1) * PATCH)
            half_ref[k * cols + j, :, :PATCH] = out[:FREQ, lanes]
            half_ref[k * cols + j, :, PATCH:] = out[FREQ:, lanes]


def correlate(rows, cols, group, sign, own_ref, other_ref, right_ref, back_ref, put,
              peak_ref, mass_ref, tilt_ref):
    row = lax.broadcasted_iota(jnp.int32, (group, FREQ, PATCH), 1)
    lane = lax.broadcasted_iota(jnp.int32, (group, FREQ, PATCH), 2)
    varies = ((row + lane) > 0).astype(jnp.float32).reshape(group * FREQ, PATCH)
    lag = lax.broadcasted_iota(jnp.int32, (PATCH, 1), 0)
    lag = jnp.where(lag < PATCH // 2, lag, lag - PATCH).astype(jnp.float32)
    for n in range(0, rows * cols, group):
        both = jnp.concatenate([ref[n:n + group].reshape(group * FREQ, 2 * PATCH) for ref in (own_ref, other_ref)])
        freq = right_dft(both, right_ref)
        first, second = freq[:group * FREQ], freq[group * FREQ:]
        re1, im1 = first[:, :PATCH] * varies, first[:, PATCH:] * varies
        re2, im2 = second[:, :PATCH] * varies, second[:, PATCH:] * varies
        cross = jnp.concatenate([re1 * re2 + im1 * im2, (im1 * re2 - re1 * im2) * sign], axis=1)
        mixed = right_dft(cross, right_ref)
        columns = []
        for m in range(group):
            part = mixed[m * FREQ:(m + 1) * FREQ]
            columns.append(jnp.concatenate([part[:, :PATCH], part[:, PATCH:]], axis=0))
        high, low = split(jnp.concatenate(columns, axis=1))
        scores = mul(back_ref[...], jnp.concatenate([high, low, high], axis=0))
        peak = jnp.max(scores, axis=0, keepdims=True)
        weight = jnp.exp(scores - peak)
        mass = jnp.sum(weight, axis=0, keepdims=True)
        tilt = jnp.sum(weight * lag, axis=0, keepdims=True)
        for m in range(group):
            lanes = slice(m * PATCH, (m + 1) * PATCH)
            peak_ref[n + m:n + m + 1, :] = peak[:, lanes]
            mass_ref[n + m:n + m + 1, :] = mass[:, lanes]
            tilt_ref[n + m:n + m + 1, :] = tilt[:, lanes]
    peak = peak_ref[...]
    share = jnp.exp(peak - jnp.max(peak, axis=1, keepdims=True))
    mass = mass_ref[...] * share
    lag = lax.broadcasted_iota(jnp.int32, mass.shape, 1)
    place = lax.broadcasted_iota(jnp.int32, mass.shape, 0) % cols
    here = lag == place
    lag = jnp.where(lag < PATCH // 2, lag, lag - PATCH).astype(jnp.float32)
    total = jnp.sum(mass, axis=1, keepdims=True)
    flow_y = jnp.sum(tilt_ref[...] * share, axis=1, keepdims=True) / total
    flow_x = jnp.sum(mass * lag, axis=1, keepdims=True) / total
    for c, value in enumerate((flow_y, flow_x)):
        spread = jnp.where(here, value, 0.0)
        for i in range(rows):
            put(c, i, jnp.sum(spread[i * cols:(i + 1) * cols], axis=0, keepdims=True))


def flow_kernel(rows, cols, group, region_ref, left_ref, right_ref, back_ref, flow_ref,
                high_ref, low_ref, own_ref, other_ref, *stats):
    for z, half_ref in enumerate((own_ref, other_ref)):
        keep_region(region_ref[z], cols * STRIDE, high_ref, low_ref)
        left_dft(cols, range(rows), high_ref, low_ref, left_ref, half_ref)

    def put(c, i, row):
        flow_ref[c * rows + i:c * rows + i + 1, :] = row

    correlate(rows, cols, group, 1.0, own_ref, other_ref, right_ref, back_ref, put, *stats)


def region_scratch(rows, cols):
    return [pltpu.VMEM(((rows + 1) * STRIDE, 2 * cols * STRIDE), jnp.bfloat16)] * 2


def half_shape(rows, cols):
    return (rows * cols, FREQ, 2 * PATCH)


def stats_scratch(rows, cols):
    return [pltpu.VMEM((rows * cols, PATCH), jnp.float32)] * 3


IN_VMEM = pl.BlockSpec(memory_space=pltpu.VMEM)


def kernel_call(body, outs, *args, scratch=(), last=False):
    args = [pltpu.with_memory_space_constraint(a, pltpu.VMEM) if isinstance(a, jax.Array) else a for a in args]
    shapes = outs if last else jax.tree.map(lambda out: pltpu.VMEM(out.shape, out.dtype), outs)
    return pl.pallas_call(
        body,
        out_shape=shapes,
        in_specs=[IN_VMEM] * len(args),
        out_specs=jax.tree.map(lambda _: IN_VMEM, outs),
        scratch_shapes=scratch,
        compiler_params=pltpu.CompilerParams(vmem_limit_bytes=24 << 20),
    )(*args)


def floats(*shape):
    return jax.ShapeDtypeStruct(shape, jnp.float32)


def flow_of(region, rows, cols, group=4):
    return kernel_call(
        functools.partial(flow_kernel, rows, cols, group),
        floats(2 * rows, PATCH), region, *tables(),
        scratch=region_scratch(rows, cols) + [pltpu.VMEM(half_shape(rows, cols), jnp.float32)] * 2
        + stats_scratch(rows, cols),
    )


def shifted(value, axis, by):
    length = lax.axis_size(axis)
    pairs = [(i, i + by) for i in range(length) if 0 <= i + by < length]
    return lax.ppermute(value, axis, pairs)


def padded_2(value, sides, width):
    for axis, dim in sides:
        size, length = (lax.axis_size(axis), value.shape[dim])
        up = [(i, (i + 1) % size) for i in range(size - 1)]
        down = [(j, i) for i, j in up]
        last = lax.slice_in_dim(value, length - width, length, axis=dim)
        first = lax.slice_in_dim(value, 0, width, axis=dim)
        before = lax.ppermute(last, axis, up)
        after = lax.ppermute(first, axis, down)
        value = jnp.concatenate([before, value, after], axis=dim)
    return value


def lap_of(padded, center):
    return (
        padded[:, :-2, 1:-1]
        + padded[:, 2:, 1:-1]
        + padded[:, 1:-1, :-2]
        + padded[:, 1:-1, 2:]
        - 4.0 * center
    )


def whole_sections(images):
    tile = images[0]
    rows, cols = tile.shape[0] // STRIDE, tile.shape[1] // STRIDE
    region = padded_2(jnp.stack([tile, shifted(tile, "sec", -1)]), (("ty", 1), ("tx", 2)), HALF)
    flow = flow_of(region, rows, cols)[:, :cols].reshape(2, rows, cols)
    keep = (lax.axis_index("sec") < lax.axis_size("sec") - 1).astype(jnp.float32)
    flow = flow * keep
    padded = padded_2(flow, (("ty", 1), ("tx", 2)), 2)
    inner = padded[:, 1:-1, 1:-1]
    first = inner + rate * (stiffness * lap_of(padded, inner) + inner - inner)
    row_ids = lax.axis_index("ty") * rows + jnp.arange(-1, rows + 1, dtype=jnp.int32)
    col_ids = lax.axis_index("tx") * cols + jnp.arange(-1, cols + 1, dtype=jnp.int32)
    row_ok = (row_ids >= 0) & (row_ids < rows * lax.axis_size("ty"))
    col_ok = (col_ids >= 0) & (col_ids < cols * lax.axis_size("tx"))
    first = first * (row_ok[:, None] & col_ok[None, :]).astype(jnp.float32)[None]
    center = first[:, 1:-1, 1:-1]
    mesh = center + rate * (stiffness * lap_of(first, center) + flow - center)
    everything = lax.all_gather(mesh, "sec")
    earlier = jnp.arange(lax.axis_size("sec")) < lax.axis_index("sec")
    before = jnp.sum(jnp.where(earlier[:, None, None, None], everything, 0.0), axis=0)
    return (mesh[None], before[None])


AXES = ("sec", "ty", "tx")


def placed(half, y, x):
    ny, nx = lax.axis_size("ty"), lax.axis_size("tx")
    return (((half + x) % 2) * ny + y) * nx + x


def along(value, step):
    ny, nx = lax.axis_size("ty"), lax.axis_size("tx")
    pairs = []
    for y in range(ny):
        for g in range(2 * nx):
            to = step(g) % (2 * nx)
            pairs.append((placed(g % 2, y, g // 2), placed(to % 2, y, to // 2)))
    return lax.ppermute(value, AXES, pairs)


def mate(g):
    return g ^ 1


def near(g):
    return g - 1 if g % 2 == 0 else g + 1


def far(g):
    return g - 2 if g % 2 == 0 else g + 2


def past(g):
    return g + 2 if g % 2 == 0 else g - 2


def pairs_even(value):
    size = lax.axis_size("ty")
    return lax.ppermute(value, "ty", [(i, i ^ 1) for i in range(size)])


def pairs_odd(value):
    size = lax.axis_size("ty")
    return lax.ppermute(value, "ty", [(i, (i - 1 if i % 2 == 0 else i + 1) % size) for i in range(size)])


def around(y, ny, even, odd):
    lower = y % 2 == 1
    above = jnp.where(y == 0, 0.0, jnp.where(lower, even, odd))
    below = jnp.where(y == ny - 1, 0.0, jnp.where(lower, odd, even))
    return above, below


def where_am_i():
    section, y, x = lax.axis_index("sec"), lax.axis_index("ty"), lax.axis_index("tx")
    return section, y, x, (section + x) % 2


def stack_rows(parts, start, stop):
    taken, base = [], 0
    for height, rows in parts:
        low, high = max(start - base, 0), min(stop - base, height)
        if low < high:
            taken.append(rows(low, high))
        base += height
    return taken[0] if len(taken) == 1 else jnp.concatenate(taken, axis=0)


def cut_kernel(core, upper, tile_ref, out_ref, even_ref, odd_ref):
    _, y, _, half = where_am_i()
    tall, width = tile_ref.shape

    @pl.when(half == 0)
    def _():
        out_ref[...] = tile_ref[:upper, width - core:]

    @pl.when(half == 1)
    def _():
        out_ref[...] = tile_ref[:upper, :core]

    first, last = tile_ref[:HALF], tile_ref[tall - HALF:]
    lower = y % 2 == 1
    even_ref[...] = jnp.where(lower, first, last)
    odd_ref[...] = jnp.where(lower, last, first)


def packed(column):
    quarter = column.shape[0] // 4
    return jnp.concatenate([column[q * quarter:(q + 1) * quarter] for q in range(4)], axis=1)


def unpacked(block):
    return jnp.concatenate([block[:, q * HALF:(q + 1) * HALF] for q in range(4)], axis=0)


def borders_kernel(core, upper, ny, tile_ref, even_ref, odd_ref, above_ref, rest_ref, near_ref, past_ref):
    _, y, _, half = where_am_i()
    width = tile_ref.shape[1]
    above, below = around(y, ny, even_ref[...], odd_ref[...])

    def column(lanes):
        return packed(jnp.concatenate([above[:, lanes], tile_ref[:, lanes], below[:, lanes]], axis=0))

    start, end = slice(0, HALF), slice(width - HALF, width)
    first, last = column(start), column(end)

    def send(lanes):
        above_ref[...] = above[:, lanes]
        rest_ref[...] = jnp.concatenate([tile_ref[upper:, lanes], below[:, lanes]], axis=0)

    @pl.when(half == 0)
    def _():
        send(slice(width - core, width))
        near_ref[...], past_ref[...] = first, last

    @pl.when(half == 1)
    def _():
        send(slice(0, core))
        near_ref[...], past_ref[...] = last, first


def fill_region(values, side, first_row, rows, cols, half, high_ref, low_ref):
    start, stop = first_row * STRIDE, (first_row + rows + 1) * STRIDE

    @pl.when(half == 0)
    def _():
        value = jnp.concatenate([side[start:stop], values(0, start, stop)], axis=1)
        keep_region(value, cols * STRIDE, high_ref, low_ref)

    @pl.when(half == 1)
    def _():
        value = jnp.concatenate([values(1, start, stop), side[start:stop]], axis=1)
        keep_region(value, cols * STRIDE, high_ref, low_ref)


def own_values(core, tile_ref, above, below):
    tall, width = tile_ref.shape

    def values(h, start, stop):
        lanes = slice(0, core) if h == 0 else slice(width - core, width)
        parts = [(HALF, lambda low, high: above[low:high, lanes]),
                 (tall, lambda low, high: tile_ref[low:high, lanes]),
                 (HALF, lambda low, high: below[low:high, lanes])]
        return stack_rows(parts, start, stop)

    return values


def other_values(refs):
    parts = [(ref.shape[0], lambda low, high, ref=ref: ref[low:high]) for ref in refs]
    return lambda h, start, stop: stack_rows(parts, start, stop)


def upper_kernel(early, rows, cols, group, ny, nx, tile_ref, even_ref, odd_ref, side_ref,
                 above_ref, other_ref, cross_ref, left_ref, right_ref, back_ref, flow_ref, later_ref,
                 own_high, own_low, high_ref, low_ref, own_half, other_half, *stats):
    section, y, x, half = where_am_i()
    at_end = jnp.where(half == 0, x == 0, x == nx - 1)
    above, below = around(y, ny, even_ref[...], odd_ref[...])
    side = jnp.where(at_end, 0.0, unpacked(side_ref[...]))
    fill_region(own_values(other_ref.shape[1], tile_ref, above, below), side, 0, rows, cols, half, own_high, own_low)
    left_dft(cols, range(early), own_high, own_low, left_ref, own_half)
    left_dft(cols, range(early, rows), own_high, own_low, left_ref, later_ref)
    side = jnp.where(at_end, 0.0, unpacked(cross_ref[...]))
    fill_region(other_values([above_ref, other_ref]), side, 0, early, cols, half, high_ref, low_ref)
    left_dft(cols, range(early), high_ref, low_ref, left_ref, other_half)
    flow_ref[...] = jnp.zeros_like(flow_ref)

    def put(c, i, row):
        flow_ref[c * rows + i:c * rows + i + 1, :] = row

    sign = jnp.where(section == 0, 1.0, -1.0)
    correlate(early, cols, group, sign, own_half, other_half, right_ref, back_ref, put, *stats)


def lower_kernel(early, rows, cols, group, nx, later_ref, above_ref, other_ref, rest_ref, cross_ref,
                 before_ref, left_ref, right_ref, back_ref, flow_ref, high_ref, low_ref, other_half, *stats):
    section, _, x, half = where_am_i()
    at_end = jnp.where(half == 0, x == 0, x == nx - 1)
    side = jnp.where(at_end, 0.0, unpacked(cross_ref[...]))
    others = other_values([above_ref, other_ref, rest_ref])
    fill_region(others, side, early, rows - early, cols, half, high_ref, low_ref)
    left_dft(cols, range(rows - early), high_ref, low_ref, left_ref, other_half)
    flow_ref[...] = before_ref[...]

    def put(c, i, row):
        at = c * rows + early + i
        flow_ref[at:at + 1, :] = row

    sign = jnp.where(section == 0, 1.0, -1.0)
    correlate(rows - early, cols, group, sign, later_ref, other_half, right_ref, back_ref, put, *stats)


def window_kernel(width, nx, own_ref, mate_ref, near_ref, far_ref, out_ref):
    _, _, x, place = where_am_i()
    half = place == 1
    own, other, close, beyond = own_ref[...], mate_ref[...], near_ref[...], far_ref[...]
    lane = lax.broadcasted_iota(jnp.int32, own.shape, 1)
    begin = jnp.where(x == 0, 0.0, jnp.where(half, beyond, close))
    left = jnp.where(half, other, own)
    right = jnp.where(half, own, other)
    end = jnp.where(x == nx - 1, 0.0, jnp.where(half, close, beyond))
    begin, left = pltpu.roll(begin, PATCH + 2 - width, 1), pltpu.roll(left, 2, 1)
    right, end = pltpu.roll(right, 2 + width, 1), pltpu.roll(end, 2 + 2 * width, 1)
    value = jnp.where(lane < 2, begin, jnp.where(lane < 2 + width, left, right))
    value = jnp.where(lane < 2 + 2 * width, value, jnp.where(lane < 4 + 2 * width, end, 0.0))
    out_ref[...] = value


def relax_kernel(rows, cols, ny, nx, own_ref, even_ref, odd_ref, mesh_ref, earlier_ref):
    section, y, x, _ = where_am_i()
    above, below = around(y, ny, even_ref[...], odd_ref[...])
    own = own_ref[...]
    tall = rows + 4
    shape = (tall, PATCH)
    row = lax.broadcasted_iota(jnp.int32, shape, 0) - 2 + y * rows
    col = lax.broadcasted_iota(jnp.int32, shape, 1) - 2 + x * cols
    inside = (row >= 0) & (row < ny * rows) & (col >= 0) & (col < nx * cols)

    def step(mesh, flow):
        nearby = (
            pltpu.roll(mesh, 1, 0) + pltpu.roll(mesh, tall - 1, 0)
            + pltpu.roll(mesh, 1, 1) + pltpu.roll(mesh, PATCH - 1, 1)
        )
        lap = nearby - 4.0 * mesh
        return jnp.where(inside, mesh + rate * (stiffness * lap + flow - mesh), 0.0)

    for c in range(2):
        flow = jnp.concatenate(
            [above[(c + 1) * rows - 2:(c + 1) * rows], own[c * rows:(c + 1) * rows],
             below[c * rows:c * rows + 2]], axis=0)
        flow = jnp.where(inside, flow, 0.0)
        mesh = step(step(flow, flow), flow)
        mesh = pltpu.roll(pltpu.roll(mesh, tall - 2, 0), PATCH - 2, 1)[:rows, :cols]
        mesh_ref[0, c] = jnp.where(section == 0, mesh, 0.0)
        earlier_ref[0, c] = jnp.where(section == 0, 0.0, mesh)


def shared_section(images):
    tile = images[0]
    ny, nx = lax.axis_size("ty"), lax.axis_size("tx")
    rows, cols = tile.shape[0] // STRIDE, tile.shape[1] // STRIDE
    half, early = cols // 2, rows // 2
    core, upper = half * STRIDE + HALF, early * STRIDE + HALF
    tall = tile.shape[0] + 2 * HALF

    strip = floats(HALF, tile.shape[1])
    payload, even, odd = kernel_call(
        functools.partial(cut_kernel, core, upper), (floats(upper, core), strip, strip), tile,
    )
    other = along(payload, mate)
    even, odd = pairs_even(even), pairs_odd(odd)
    edge = floats(tall // 4, 4 * HALF)
    above, rest, edge_near, edge_past = kernel_call(
        functools.partial(borders_kernel, core, upper, ny),
        (floats(HALF, core), floats(tile.shape[0] - upper + HALF, core), edge, edge),
        tile, even, odd,
    )
    above, side = along(above, mate), along(edge_near, near)
    cross, rest = along(edge_past, past), along(rest, mate)
    constants = tables()
    half_of = lambda count: pltpu.VMEM(half_shape(count, half), jnp.float32)
    late = rows - early
    flow, later = kernel_call(
        functools.partial(upper_kernel, early, rows, half, 4, ny, nx),
        (floats(2 * rows, PATCH), floats(*half_shape(late, half))),
        tile, even, odd, side, above, other, cross, *constants,
        scratch=region_scratch(rows, half) + region_scratch(early, half) + [half_of(early)] * 2
        + stats_scratch(early, half),
    )
    flow = kernel_call(
        functools.partial(lower_kernel, early, rows, half, 4, nx), floats(2 * rows, PATCH),
        later, above, other, rest, cross, flow, *constants,
        scratch=region_scratch(late, half) + [half_of(late)] + stats_scratch(late, half),
    )
    window = kernel_call(
        functools.partial(window_kernel, half, nx), floats(*flow.shape),
        flow, along(flow, mate), along(flow, near), along(flow, far),
    )
    out = floats(1, 2, rows, cols)
    return kernel_call(
        functools.partial(relax_kernel, rows, cols, ny, nx), (out, out),
        window, pairs_even(window), pairs_odd(window), last=True,
    )


def solution(mesh):
    in_specs = (P("sec", "ty", "tx"),)
    out_specs = (P("sec", None, "ty", "tx"), P("sec", None, "ty", "tx"))
    even = mesh.shape["ty"] % 2 == 0 and mesh.shape["tx"] % 2 == 0
    shared = mesh.shape["sec"] == 2 and even

    def body(images):
        return (shared_section if shared else whole_sections)(images)

    return jax.shard_map(body, mesh=mesh, in_specs=in_specs, out_specs=out_specs, check_vma=False)
```

profile of v0, /device:TPU:0, one launch (start us, length us, event | category | flops | bytes accessed | tf_op | source)
XLA Modules:
  0.0 39.5 jit_solution(13844065945912915007)
XLA Ops:
  0.6 0.0 copy-start
  0.6 1.0 %copy-done = f32[1,256,512]{2,1,0:T(8,128)S(1)} copy-done((f32[1,256,512]{2,1,0:T(8,128)S(1)}, f32[1,256,512]{2,1,0:T(8,128)}, u32[]{:S(2)}) %copy-start) | copy-done | bytes 524312
  1.7 0.1 shard_map.59
  1.8 0.6 %collective-permute-start = (f32[32,512]{1,0:T(8,128)S(1)}, f32[32,512]{1,0:T(8,128)S(1)}, u32[]{:S(2)}, u32[]{:S(2)}) collective-permute-start(f32[32,512]{1,0:T(8,128)S(1)} %get-tuple-element.11), channel_id=1, source_target_pairs={{0,4},{4,0},{8,12},{12,8},{1,5},{5,1},{9,13},{13,9},{2,6},{6,2},{1... | collective-permute-start | bytes 196616 | tf_op jit(solution)/shard_map/ppermute | solution.py:271
  2.4 2.6 %collective-permute-start.1 = (f32[32,512]{1,0:T(8,128)S(1)}, f32[32,512]{1,0:T(8,128)S(1)}, u32[]{:S(2)}, u32[]{:S(2)}) collective-permute-start(f32[32,512]{1,0:T(8,128)S(1)} %get-tuple-element.12), channel_id=1, source_target_pairs={{0,12},{4,8},{8,4},{12,0},{1,13},{5,9},{9,5},{13,1},{2,14},{6,10},... | collective-permute-start | bytes 196616 | tf_op jit(solution)/shard_map/ppermute | solution.py:276
  5.0 0.0 copy-start.1
  5.0 0.0 copy-start.2
  5.0 0.0 copy-start.3
  5.0 1.4 %collective-permute-start.4 = (f32[160,288]{1,0:T(8,128)S(1)}, f32[160,288]{1,0:T(8,128)S(1)}, u32[]{:S(2)}, u32[]{:S(2)}) collective-permute-start(f32[160,288]{1,0:T(8,128)S(1)} %get-tuple-element.15), channel_id=1, source_target_pairs={{0,16},{16,0},{17,1},{1,17},{2,18},{18,2},{19,3},{3,19},{4,20},{20... | collective-permute-start | bytes 552968 | tf_op jit(solution)/shard_map/ppermute | solution.py:250
  6.4 0.0 collective-permute-done.even_ref
  6.4 1.0 %collective-permute-done.1.odd_ref = f32[32,512]{1,0:T(8,128)S(1)} collective-permute-done((f32[32,512]{1,0:T(8,128)S(1)}, f32[32,512]{1,0:T(8,128)S(1)}, u32[]{:S(2)}, u32[]{:S(2)}) %collective-permute-start.1) | collective-permute-done | bytes 65568 | tf_op jit(solution)/shard_map/ppermute | solution.py:276
  7.4 0.2 shard_map.60
  7.6 1.2 %collective-permute-start.6 = (f32[128,288]{1,0:T(8,128)S(1)}, f32[128,288]{1,0:T(8,128)S(1)}, u32[]{:S(2)}, u32[]{:S(2)}) collective-permute-start(f32[128,288]{1,0:T(8,128)S(1)} %get-tuple-element.18), channel_id=1, source_target_pairs={{0,16},{16,0},{17,1},{1,17},{2,18},{18,2},{19,3},{3,19},{4,20},{20... | collective-permute-start | bytes 442376 | tf_op jit(solution)/shard_map/ppermute | solution.py:250
  8.9 3.8 %collective-permute-start.2 = (f32[80,128]{1,0:T(8,128)S(1)}, f32[80,128]{1,0:T(8,128)S(1)}, u32[]{:S(2)}, u32[]{:S(2)}) collective-permute-start(f32[80,128]{1,0:T(8,128)S(1)} %get-tuple-element.13), channel_id=1, source_target_pairs={{0,3},{16,17},{17,16},{1,2},{2,1},{18,19},{19,18},{3,0},{4,7},{20,... | collective-permute-start | bytes 122888 | tf_op jit(solution)/shard_map/ppermute | solution.py:250
  12.7 0.0 collective-permute-start.5
  12.7 1.5 %collective-permute-start.3 = (f32[32,288]{1,0:T(8,128)S(1)}, f32[32,288]{1,0:T(8,128)S(1)}, u32[]{:S(2)}, u32[]{:S(2)}) collective-permute-start(f32[32,288]{1,0:T(8,128)S(1)} %get-tuple-element.14), channel_id=1, source_target_pairs={{0,16},{16,0},{17,1},{1,17},{2,18},{18,2},{19,3},{3,19},{4,20},{20... | collective-permute-start | bytes 110600 | tf_op jit(solution)/shard_map/ppermute | solution.py:250
  14.1 4.5 %collective-permute-done.3.above_ref = f32[32,288]{1,0:T(8,128)S(1)} collective-permute-done((f32[32,288]{1,0:T(8,128)S(1)}, f32[32,288]{1,0:T(8,128)S(1)}, u32[]{:S(2)}, u32[]{:S(2)}) %collective-permute-start.3) | collective-permute-done | bytes 36896 | tf_op jit(solution)/shard_map/ppermute | solution.py:250
  18.6 0.0 collective-permute-done.2.side_ref
  18.6 0.7 %collective-permute-done.5.cross_ref = f32[80,128]{1,0:T(8,128)S(1)} collective-permute-done((f32[80,128]{1,0:T(8,128)S(1)}, f32[80,128]{1,0:T(8,128)S(1)}, u32[]{:S(2)}, u32[]{:S(2)}) %collective-permute-start.5) | collective-permute-done | bytes 40992 | tf_op jit(solution)/shard_map/ppermute | solution.py:250
  19.4 0.0 collective-permute-done.4.other_ref
  19.4 0.0 copy-done.1
  19.4 0.0 copy-done.2
  19.4 0.0 copy-done.3
  19.4 3.7 %shard_map.61 = (f32[8,128]{1,0:T(8,128)S(1)}, f32[8,72,256]{2,1,0:T(8,128)S(1)}) custom-call(f32[256,512]{1,0:T(8,128)S(1)} %bitcast.3, f32[32,512]{1,0:T(8,128)S(1)} %collective-permute-done.even_ref, f32[32,512]{1,0:T(8,128)S(1)} %collective-permute-done.1.odd_ref, f32[80,128]{1,0:T(8,128)S(1)} %collective-permute-done.2.side_ref, ...), custom_call_target="tpu_custom_call" | custom-call | tf_op jit(solution)/shard_map/pallas_call | solution.py:160
  23.0 0.0 collective-permute-done.6.rest_ref
  23.1 2.8 %shard_map.62.own_ref = f32[8,128]{1,0:T(8,128)S(1)} custom-call(f32[8,72,256]{2,1,0:T(8,128)S(1)} %get-tuple-element.17.later_ref, f32[32,288]{1,0:T(8,128)S(1)} %collective-permute-done.3.above_ref, f32[160,288]{1,0:T(8,128)S(1)} %collective-permute-done.4.other_ref, f32[128,288]{1,0:T(8,128)S(1)} %collective-permute-done.6.rest_ref, ...), custom_call_target="tpu_custom_call" | custom-call | tf_op jit(solution)/shard_map/pallas_call | solution.py:160
  25.9 4.3 %collective-permute-start.9 = (f32[8,128]{1,0:T(8,128)S(1)}, f32[8,128]{1,0:T(8,128)S(1)}, u32[]{:S(2)}, u32[]{:S(2)}) collective-permute-start(f32[8,128]{1,0:T(8,128)S(1)} %shard_map.62.own_ref), channel_id=1, source_target_pairs={{0,19},{16,1},{17,0},{1,18},{2,17},{18,3},{19,2},{3,16},{4,23},{20... | collective-permute-start | bytes 12296 | tf_op jit(solution)/shard_map/ppermute | solution.py:250
  30.1 0.1 collective-permute-start.8
  30.3 0.0 collective-permute-start.7
  30.3 1.2 %collective-permute-done.9.far_ref = f32[8,128]{1,0:T(8,128)S(1)} collective-permute-done((f32[8,128]{1,0:T(8,128)S(1)}, f32[8,128]{1,0:T(8,128)S(1)}, u32[]{:S(2)}, u32[]{:S(2)}) %collective-permute-start.9) | collective-permute-done | bytes 4128 | tf_op jit(solution)/shard_map/ppermute | solution.py:250
  31.5 4.1 %collective-permute-done.8.near_ref = f32[8,128]{1,0:T(8,128)S(1)} collective-permute-done((f32[8,128]{1,0:T(8,128)S(1)}, f32[8,128]{1,0:T(8,128)S(1)}, u32[]{:S(2)}, u32[]{:S(2)}) %collective-permute-start.8) | collective-permute-done | bytes 4128 | tf_op jit(solution)/shard_map/ppermute | solution.py:250
  35.6 0.0 collective-permute-done.7.mate_ref
  35.6 0.1 shard_map.63.own_ref
  35.6 0.0 collective-permute-start.11
  35.7 0.6 %collective-permute-start.10 = (f32[8,128]{1,0:T(8,128)S(1)}, f32[8,128]{1,0:T(8,128)S(1)}, u32[]{:S(2)}, u32[]{:S(2)}) collective-permute-start(f32[8,128]{1,0:T(8,128)S(1)} %shard_map.63.own_ref), channel_id=1, source_target_pairs={{0,4},{4,0},{8,12},{12,8},{1,5},{5,1},{9,13},{13,9},{2,6},{6,2},{1... | collective-permute-start | bytes 12296 | tf_op jit(solution)/shard_map/ppermute | solution.py:271
  36.3 2.4 %collective-permute-done.11.odd_ref = f32[8,128]{1,0:T(8,128)S(1)} collective-permute-done((f32[8,128]{1,0:T(8,128)S(1)}, f32[8,128]{1,0:T(8,128)S(1)}, u32[]{:S(2)}, u32[]{:S(2)}) %collective-permute-start.11) | collective-permute-done | bytes 4128 | tf_op jit(solution)/shard_map/ppermute | solution.py:276
  38.7 0.0 collective-permute-done.10.even_ref
  38.7 0.8 %shard_map.64 = (f32[1,2,4,8]{3,2,1,0:T(4,128)}, f32[1,2,4,8]{3,2,1,0:T(4,128)}) custom-call(f32[8,128]{1,0:T(8,128)S(1)} %shard_map.63.own_ref, f32[8,128]{1,0:T(8,128)S(1)} %collective-permute-done.10.even_ref, f32[8,128]{1,0:T(8,128)S(1)} %collective-permute-done.11.odd_ref), custom_call_target="tpu_custom_call" | custom-call | tf_op jit(solution)/shard_map/pallas_call | solution.py:160
Async XLA Ops:
  0.6 1.0 %copy-start = (f32[1,256,512]{2,1,0:T(8,128)S(1)}, f32[1,256,512]{2,1,0:T(8,128)}, u32[]{:S(2)}) copy-start(f32[1,256,512]{2,1,0:T(8,128)} %param.4) | copy-start | bytes 1572868
  1.8 4.6 %collective-permute-start = (f32[32,512]{1,0:T(8,128)S(1)}, f32[32,512]{1,0:T(8,128)S(1)}, u32[]{:S(2)}, u32[]{:S(2)}) collective-permute-start(f32[32,512]{1,0:T(8,128)S(1)} %get-tuple-element.11), channel_id=1, source_target_pairs={{0,4},{4,0},{8,12},{12,8},{1,5},{5,1},{9,13},{13,9},{2,6},{6,2},{1... | collective-permute-start | bytes 196616 | tf_op jit(solution)/shard_map/ppermute | solution.py:271
  2.4 5.0 %collective-permute-start.1 = (f32[32,512]{1,0:T(8,128)S(1)}, f32[32,512]{1,0:T(8,128)S(1)}, u32[]{:S(2)}, u32[]{:S(2)}) collective-permute-start(f32[32,512]{1,0:T(8,128)S(1)} %get-tuple-element.12), channel_id=1, source_target_pairs={{0,12},{4,8},{8,4},{12,0},{1,13},{5,9},{9,5},{13,1},{2,14},{6,10},... | collective-permute-start | bytes 196616 | tf_op jit(solution)/shard_map/ppermute | solution.py:276
  5.0 14.4 %copy-start.1 = (bf16[2,256,256]{2,1,0:T(8,128)(2,1)S(1)}, bf16[2,256,256]{2,1,0:T(8,128)(2,1)}, u32[]{:S(2)}) copy-start(bf16[2,256,256]{2,1,0:T(8,128)(2,1)} %constant.7.clone.right_ref) | copy-start | bytes 786436
  5.0 14.4 %copy-start.2 = (bf16[128,432]{1,0:T(8,128)(2,1)S(1)}, bf16[128,432]{1,0:T(8,128)(2,1)}, u32[]{:S(2)}) copy-start(bf16[128,432]{1,0:T(8,128)(2,1)} %constant.8.clone.back_ref) | copy-start | bytes 331780
  5.0 14.4 %copy-start.3 = (bf16[144,384]{1,0:T(8,128)(2,1)S(1)}, bf16[144,384]{1,0:T(8,128)(2,1)}, u32[]{:S(2)}) copy-start(bf16[144,384]{1,0:T(8,128)(2,1)} %constant.6.clone.left_ref) | copy-start | bytes 331780
  5.0 14.4 %collective-permute-start.4 = (f32[160,288]{1,0:T(8,128)S(1)}, f32[160,288]{1,0:T(8,128)S(1)}, u32[]{:S(2)}, u32[]{:S(2)}) collective-permute-start(f32[160,288]{1,0:T(8,128)S(1)} %get-tuple-element.15), channel_id=1, source_target_pairs={{0,16},{16,0},{17,1},{1,17},{2,18},{18,2},{19,3},{3,19},{4,20},{20... | collective-permute-start | bytes 552968 | tf_op jit(solution)/shard_map/ppermute | solution.py:250
  7.6 15.4 %collective-permute-start.6 = (f32[128,288]{1,0:T(8,128)S(1)}, f32[128,288]{1,0:T(8,128)S(1)}, u32[]{:S(2)}, u32[]{:S(2)}) collective-permute-start(f32[128,288]{1,0:T(8,128)S(1)} %get-tuple-element.18), channel_id=1, source_target_pairs={{0,16},{16,0},{17,1},{1,17},{2,18},{18,2},{19,3},{3,19},{4,20},{20... | collective-permute-start | bytes 442376 | tf_op jit(solution)/shard_map/ppermute | solution.py:250
  8.9 9.8 %collective-permute-start.2 = (f32[80,128]{1,0:T(8,128)S(1)}, f32[80,128]{1,0:T(8,128)S(1)}, u32[]{:S(2)}, u32[]{:S(2)}) collective-permute-start(f32[80,128]{1,0:T(8,128)S(1)} %get-tuple-element.13), channel_id=1, source_target_pairs={{0,3},{16,17},{17,16},{1,2},{2,1},{18,19},{19,18},{3,0},{4,7},{20,... | collective-permute-start | bytes 122888 | tf_op jit(solution)/shard_map/ppermute | solution.py:250
  12.7 6.7 %collective-permute-start.5 = (f32[80,128]{1,0:T(8,128)S(1)}, f32[80,128]{1,0:T(8,128)S(1)}, u32[]{:S(2)}, u32[]{:S(2)}) collective-permute-start(f32[80,128]{1,0:T(8,128)S(1)} %get-tuple-element.16), channel_id=1, source_target_pairs={{0,17},{16,3},{17,2},{1,16},{2,19},{18,1},{19,0},{3,18},{4,21},{20... | collective-permute-start | bytes 122888 | tf_op jit(solution)/shard_map/ppermute | solution.py:250
  12.7 6.0 %collective-permute-start.3 = (f32[32,288]{1,0:T(8,128)S(1)}, f32[32,288]{1,0:T(8,128)S(1)}, u32[]{:S(2)}, u32[]{:S(2)}) collective-permute-start(f32[32,288]{1,0:T(8,128)S(1)} %get-tuple-element.14), channel_id=1, source_target_pairs={{0,16},{16,0},{17,1},{1,17},{2,18},{18,2},{19,3},{3,19},{4,20},{20... | collective-permute-start | bytes 110600 | tf_op jit(solution)/shard_map/ppermute | solution.py:250
  25.9 5.6 %collective-permute-start.9 = (f32[8,128]{1,0:T(8,128)S(1)}, f32[8,128]{1,0:T(8,128)S(1)}, u32[]{:S(2)}, u32[]{:S(2)}) collective-permute-start(f32[8,128]{1,0:T(8,128)S(1)} %shard_map.62.own_ref), channel_id=1, source_target_pairs={{0,19},{16,1},{17,0},{1,18},{2,17},{18,3},{19,2},{3,16},{4,23},{20... | collective-permute-start | bytes 12296 | tf_op jit(solution)/shard_map/ppermute | solution.py:250
  30.1 5.4 %collective-permute-start.8 = (f32[8,128]{1,0:T(8,128)S(1)}, f32[8,128]{1,0:T(8,128)S(1)}, u32[]{:S(2)}, u32[]{:S(2)}) collective-permute-start(f32[8,128]{1,0:T(8,128)S(1)} %shard_map.62.own_ref), channel_id=1, source_target_pairs={{0,3},{16,17},{17,16},{1,2},{2,1},{18,19},{19,18},{3,0},{4,7},{20,... | collective-permute-start | bytes 12296 | tf_op jit(solution)/shard_map/ppermute | solution.py:250
  30.3 5.3 %collective-permute-start.7 = (f32[8,128]{1,0:T(8,128)S(1)}, f32[8,128]{1,0:T(8,128)S(1)}, u32[]{:S(2)}, u32[]{:S(2)}) collective-permute-start(f32[8,128]{1,0:T(8,128)S(1)} %shard_map.62.own_ref), channel_id=1, source_target_pairs={{0,16},{16,0},{17,1},{1,17},{2,18},{18,2},{19,3},{3,19},{4,20},{20... | collective-permute-start | bytes 12296 | tf_op jit(solution)/shard_map/ppermute | solution.py:250
  35.6 3.0 %collective-permute-start.11 = (f32[8,128]{1,0:T(8,128)S(1)}, f32[8,128]{1,0:T(8,128)S(1)}, u32[]{:S(2)}, u32[]{:S(2)}) collective-permute-start(f32[8,128]{1,0:T(8,128)S(1)} %shard_map.63.own_ref), channel_id=1, source_target_pairs={{0,12},{4,8},{8,4},{12,0},{1,13},{5,9},{9,5},{13,1},{2,14},{6,10},... | collective-permute-start | bytes 12296 | tf_op jit(solution)/shard_map/ppermute | solution.py:276
  35.7 3.0 %collective-permute-start.10 = (f32[8,128]{1,0:T(8,128)S(1)}, f32[8,128]{1,0:T(8,128)S(1)}, u32[]{:S(2)}, u32[]{:S(2)}) collective-permute-start(f32[8,128]{1,0:T(8,128)S(1)} %shard_map.63.own_ref), channel_id=1, source_target_pairs={{0,4},{4,0},{8,12},{12,8},{1,5},{5,1},{9,13},{13,9},{2,6},{6,2},{1... | collective-permute-start | bytes 12296 | tf_op jit(solution)/shard_map/ppermute | solution.py:271
where the time goes:
time: 39.7 us; the launch traced here: 39.5 us
  starting transfers between devices  16.1 us (41%)
  waiting for transfers between devices  13.9 us (35%)
  Pallas kernels  7.76 us (20%)
  local copies, waits for them, and re-layouts  1.05 us (3%)
  between operations  0.7 us (2%)
    ppermute x8, starting transfers between devices, along(): return lax.ppermute(value, AXES, pairs)  12.3 us
    ppermute x8, waiting for transfers between devices, along(): return lax.ppermute(value, AXES, pairs)  10.5 us
    pallas_call x6, Pallas kernels, kernel_call(): pl.pallas_call(body, out_shape=shapes, in_specs=[IN_VMEM] * len(args), ou...  7.76 us
    ppermute x2, waiting for transfers between devices, pairs_odd(): lax.ppermute(value, 'ty', [(i, (i - 1 if i % 2 == 0 else i + 1) % size) f...  3.35 us
    ppermute x2, starting transfers between devices, pairs_odd(): lax.ppermute(value, 'ty', [(i, (i - 1 if i % 2 == 0 else i + 1) % size) f...  2.6 us
    ppermute x2, starting transfers between devices, pairs_even(): return lax.ppermute(value, 'ty', [(i, i ^ 1) for i in range(size)])  1.2 us
    unnamed x8, local copies, waits for them, and re-layouts  1.05 us
  transfers between devices with their start and end apart: 12, of which 6 were waited for; matrix products, arithmetic and copies ran while one was open for 0% of the time, Pallas kernels for 10%

commit v1 on v0

--- a/solution.py
+++ b/solution.py
@@ -262,10 +262,6 @@
     return g - 2 if g % 2 == 0 else g + 2
 
 
-def past(g):
-    return g + 2 if g % 2 == 0 else g - 2
-
-
 def pairs_even(value):
     size = lax.axis_size("ty")
     return lax.ppermute(value, "ty", [(i, i ^ 1) for i in range(size)])
@@ -288,34 +284,6 @@
     return section, y, x, (section + x) % 2
 
 
-def stack_rows(parts, start, stop):
-    taken, base = [], 0
-    for height, rows in parts:
-        low, high = max(start - base, 0), min(stop - base, height)
-        if low < high:
-            taken.append(rows(low, high))
-        base += height
-    return taken[0] if len(taken) == 1 else jnp.concatenate(taken, axis=0)
-
-
-def cut_kernel(core, upper, tile_ref, out_ref, even_ref, odd_ref):
-    _, y, _, half = where_am_i()
-    tall, width = tile_ref.shape
-
-    @pl.when(half == 0)
-    def _():
-        out_ref[...] = tile_ref[:upper, width - core:]
-
-    @pl.when(half == 1)
-    def _():
-        out_ref[...] = tile_ref[:upper, :core]
-
-    first, last = tile_ref[:HALF], tile_ref[tall - HALF:]
-    lower = y % 2 == 1
-    even_ref[...] = jnp.where(lower, first, last)
-    odd_ref[...] = jnp.where(lower, last, first)
-
-
 def packed(column):
     quarter = column.shape[0] // 4
     return jnp.concatenate([column[q * quarter:(q + 1) * quarter] for q in range(4)], axis=1)
@@ -325,102 +293,130 @@
     return jnp.concatenate([block[:, q * HALF:(q + 1) * HALF] for q in range(4)], axis=0)
 
 
-def borders_kernel(core, upper, ny, tile_ref, even_ref, odd_ref, above_ref, rest_ref, near_ref, past_ref):
+def packed_wide(value):
+    full = value.shape[1] // PATCH
+    tiles = [value[:, t * PATCH:(t + 1) * PATCH] for t in range(full)]
+    return jnp.concatenate(tiles + [packed(value[:, full * PATCH:])], axis=0)
+
+
+def unpacked_wide(block, tall, width):
+    full = width // PATCH
+    tiles = [block[t * tall:(t + 1) * tall] for t in range(full)]
+    return jnp.concatenate(tiles + [unpacked(block[full * tall:full * tall + tall // 4])], axis=1)
+
+
+def own_lanes(half, core, width):
+    return slice(0, core) if half == 0 else slice(width - core, width)
+
+
+def edge_of(half, value):
+    return value[:, :HALF] if half == 0 else value[:, value.shape[1] - HALF:]
+
+
+def body_of(half, value):
+    return value[:, HALF:] if half == 0 else value[:, :value.shape[1] - HALF]
+
+
+def by_half(half, branch):
+    for h in range(2):
+        pl.when(half == h)(functools.partial(branch, h))
+
+
+def cut_kernel(core, tile_ref, frame_ref, rest_ref):
+    _, _, _, half = where_am_i()
+    tall, width = tile_ref.shape
+
+    def branch(h):
+        value = tile_ref[:, own_lanes(1 - h, core, width)]
+        middle = value[HALF:tall - HALF]
+        ends = jnp.concatenate([value[:HALF], value[tall - HALF:]], axis=0)
+        frame_ref[...] = jnp.concatenate([packed_wide(ends), packed(edge_of(1 - h, middle))], axis=0)
+        rest_ref[...] = body_of(1 - h, middle)
+
+    by_half(half, branch)
+
+
+def ends_of(core, frame):
+    return unpacked_wide(frame, 2 * HALF, core)
+
+
+def side_of(tall, frame):
+    return unpacked(frame[frame.shape[0] - (tall - 2 * HALF) // 4:])
+
+
+def strips_kernel(core, tile_ref, frame_ref, even_ref, odd_ref):
     _, y, _, half = where_am_i()
-    width = tile_ref.shape[1]
+    tall, width = tile_ref.shape
+    lower = y % 2 == 1
+    ends = ends_of(core, frame_ref[...])
+
+    def branch(h):
+        lanes = own_lanes(h, core, width)
+        first = packed_wide(jnp.concatenate([tile_ref[:HALF, lanes], ends[:HALF]], axis=0))
+        last = packed_wide(jnp.concatenate([tile_ref[tall - HALF:, lanes], ends[HALF:]], axis=0))
+        even_ref[...] = jnp.where(lower, first, last)
+        odd_ref[...] = jnp.where(lower, last, first)
+
+    by_half(half, branch)
+
+
+def strips_of(core, y, ny, even_ref, odd_ref):
     above, below = around(y, ny, even_ref[...], odd_ref[...])
-
-    def column(lanes):
-        return packed(jnp.concatenate([above[:, lanes], tile_ref[:, lanes], below[:, lanes]], axis=0))
-
-    start, end = slice(0, HALF), slice(width - HALF, width)
-    first, last = column(start), column(end)
-
-    def send(lanes):
-        above_ref[...] = above[:, lanes]
-        rest_ref[...] = jnp.concatenate([tile_ref[upper:, lanes], below[:, lanes]], axis=0)
-
-    @pl.when(half == 0)
-    def _():
-        send(slice(width - core, width))
-        near_ref[...], past_ref[...] = first, last
-
-    @pl.when(half == 1)
-    def _():
-        send(slice(0, core))
-        near_ref[...], past_ref[...] = last, first
-
-
-def fill_region(values, side, first_row, rows, cols, half, high_ref, low_ref):
-    start, stop = first_row * STRIDE, (first_row + rows + 1) * STRIDE
-
-    @pl.when(half == 0)
-    def _():
-        value = jnp.concatenate([side[start:stop], values(0, start, stop)], axis=1)
-        keep_region(value, cols * STRIDE, high_ref, low_ref)
-
-    @pl.when(half == 1)
-    def _():
-        value = jnp.concatenate([values(1, start, stop), side[start:stop]], axis=1)
-        keep_region(value, cols * STRIDE, high_ref, low_ref)
-
-
-def own_values(core, tile_ref, above, below):
+    return unpacked_wide(above, 2 * HALF, core), unpacked_wide(below, 2 * HALF, core)
+
+
+def sides_kernel(core, ny, tile_ref, frame_ref, even_ref, odd_ref, side_ref):
+    _, y, _, half = where_am_i()
     tall, width = tile_ref.shape
-
-    def values(h, start, stop):
-        lanes = slice(0, core) if h == 0 else slice(width - core, width)
-        parts = [(HALF, lambda low, high: above[low:high, lanes]),
-                 (tall, lambda low, high: tile_ref[low:high, lanes]),
-                 (HALF, lambda low, high: below[low:high, lanes])]
-        return stack_rows(parts, start, stop)
-
-    return values
-
-
-def other_values(refs):
-    parts = [(ref.shape[0], lambda low, high, ref=ref: ref[low:high]) for ref in refs]
-    return lambda h, start, stop: stack_rows(parts, start, stop)
-
-
-def upper_kernel(early, rows, cols, group, ny, nx, tile_ref, even_ref, odd_ref, side_ref,
-                 above_ref, other_ref, cross_ref, left_ref, right_ref, back_ref, flow_ref, later_ref,
-                 own_high, own_low, high_ref, low_ref, own_half, other_half, *stats):
+    above, below = strips_of(core, y, ny, even_ref, odd_ref)
+    ends, side = ends_of(core, frame_ref[...]), side_of(tall, frame_ref[...])
+
+    def branch(h):
+        own = edge_of(h, tile_ref[:, own_lanes(h, core, width)])
+        over, under = edge_of(h, above), edge_of(h, below)
+        limits = edge_of(h, ends)
+        side_ref[...] = jnp.concatenate(
+            [packed(jnp.concatenate([over[:HALF], own, under[:HALF]], axis=0)),
+             packed(jnp.concatenate([over[HALF:], limits[:HALF], side, limits[HALF:], under[HALF:]], axis=0))],
+            axis=0)
+
+    by_half(half, branch)
+
+
+def shared_kernel(rows, cols, group, ny, nx, tile_ref, frame_ref, rest_ref, even_ref, odd_ref, sides_ref,
+                  left_ref, right_ref, back_ref, flow_ref, high_ref, low_ref, own_half, other_half, *stats):
     section, y, x, half = where_am_i()
+    tall, width = tile_ref.shape
+    core = cols * STRIDE + HALF
+    above, below = strips_of(core, y, ny, even_ref, odd_ref)
+    ends, side = ends_of(core, frame_ref[...]), side_of(tall, frame_ref[...])
     at_end = jnp.where(half == 0, x == 0, x == nx - 1)
-    above, below = around(y, ny, even_ref[...], odd_ref[...])
-    side = jnp.where(at_end, 0.0, unpacked(side_ref[...]))
-    fill_region(own_values(other_ref.shape[1], tile_ref, above, below), side, 0, rows, cols, half, own_high, own_low)
-    left_dft(cols, range(early), own_high, own_low, left_ref, own_half)
-    left_dft(cols, range(early, rows), own_high, own_low, left_ref, later_ref)
-    side = jnp.where(at_end, 0.0, unpacked(cross_ref[...]))
-    fill_region(other_values([above_ref, other_ref]), side, 0, early, cols, half, high_ref, low_ref)
-    left_dft(cols, range(early), high_ref, low_ref, left_ref, other_half)
-    flow_ref[...] = jnp.zeros_like(flow_ref)
+    sides = jnp.where(at_end, 0.0, sides_ref[...])
+    quarter = sides.shape[0] // 2
+    own_side, other_side = unpacked(sides[:quarter]), unpacked(sides[quarter:])
+
+    def joined(h, outer, value):
+        return jnp.concatenate([outer, value] if h == 0 else [value, outer], axis=1)
+
+    def own_branch(h):
+        middle = tile_ref[:, own_lanes(h, core, width)]
+        value = jnp.concatenate([above[:HALF], middle, below[:HALF]], axis=0)
+        keep_region(joined(h, own_side, value), cols * STRIDE, high_ref, low_ref)
+
+    def other_branch(h):
+        middle = joined(h, side, rest_ref[...])
+        value = jnp.concatenate([above[HALF:], ends[:HALF], middle, ends[HALF:], below[HALF:]], axis=0)
+        keep_region(joined(h, other_side, value), cols * STRIDE, high_ref, low_ref)
+
+    for branch, half_ref in ((own_branch, own_half), (other_branch, other_half)):
+        by_half(half, branch)
+        left_dft(cols, range(rows), high_ref, low_ref, left_ref, half_ref)
 
     def put(c, i, row):
         flow_ref[c * rows + i:c * rows + i + 1, :] = row
 
     sign = jnp.where(section == 0, 1.0, -1.0)
-    correlate(early, cols, group, sign, own_half, other_half, right_ref, back_ref, put, *stats)
-
-
-def lower_kernel(early, rows, cols, group, nx, later_ref, above_ref, other_ref, rest_ref, cross_ref,
-                 before_ref, left_ref, right_ref, back_ref, flow_ref, high_ref, low_ref, other_half, *stats):
-    section, _, x, half = where_am_i()
-    at_end = jnp.where(half == 0, x == 0, x == nx - 1)
-    side = jnp.where(at_end, 0.0, unpacked(cross_ref[...]))
-    others = other_values([above_ref, other_ref, rest_ref])
-    fill_region(others, side, early, rows - early, cols, half, high_ref, low_ref)
-    left_dft(cols, range(rows - early), high_ref, low_ref, left_ref, other_half)
-    flow_ref[...] = before_ref[...]
-
-    def put(c, i, row):
-        at = c * rows + early + i
-        flow_ref[at:at + 1, :] = row
-
-    sign = jnp.where(section == 0, 1.0, -1.0)
-    correlate(rows - early, cols, group, sign, later_ref, other_half, right_ref, back_ref, put, *stats)
+    correlate(rows, cols, group, sign, own_half, other_half, right_ref, back_ref, put, *stats)
 
 
 def window_kernel(width, nx, own_ref, mate_ref, near_ref, far_ref, out_ref):
@@ -472,38 +468,28 @@
     tile = images[0]
     ny, nx = lax.axis_size("ty"), lax.axis_size("tx")
     rows, cols = tile.shape[0] // STRIDE, tile.shape[1] // STRIDE
-    half, early = cols // 2, rows // 2
-    core, upper = half * STRIDE + HALF, early * STRIDE + HALF
-    tall = tile.shape[0] + 2 * HALF
-
-    strip = floats(HALF, tile.shape[1])
-    payload, even, odd = kernel_call(
-        functools.partial(cut_kernel, core, upper), (floats(upper, core), strip, strip), tile,
-    )
-    other = along(payload, mate)
+    half = cols // 2
+    core, tall = half * STRIDE + HALF, tile.shape[0]
+
+    wide = 2 * HALF * core // PATCH
+    strip = floats(wide, PATCH)
+    frame, rest = kernel_call(
+        functools.partial(cut_kernel, core),
+        (floats(wide + (tall - 2 * HALF) // 4, PATCH), floats(tall - 2 * HALF, core - HALF)), tile,
+    )
+    frame, rest = along(frame, mate), along(rest, mate)
+    even, odd = kernel_call(functools.partial(strips_kernel, core), (strip, strip), tile, frame)
     even, odd = pairs_even(even), pairs_odd(odd)
-    edge = floats(tall // 4, 4 * HALF)
-    above, rest, edge_near, edge_past = kernel_call(
-        functools.partial(borders_kernel, core, upper, ny),
-        (floats(HALF, core), floats(tile.shape[0] - upper + HALF, core), edge, edge),
-        tile, even, odd,
-    )
-    above, side = along(above, mate), along(edge_near, near)
-    cross, rest = along(edge_past, past), along(rest, mate)
-    constants = tables()
-    half_of = lambda count: pltpu.VMEM(half_shape(count, half), jnp.float32)
-    late = rows - early
-    flow, later = kernel_call(
-        functools.partial(upper_kernel, early, rows, half, 4, ny, nx),
-        (floats(2 * rows, PATCH), floats(*half_shape(late, half))),
-        tile, even, odd, side, above, other, cross, *constants,
-        scratch=region_scratch(rows, half) + region_scratch(early, half) + [half_of(early)] * 2
-        + stats_scratch(early, half),
-    )
+    sides = kernel_call(
+        functools.partial(sides_kernel, core, ny), floats((tall + 2 * HALF) // 2, PATCH),
+        tile, frame, even, odd,
+    )
+    sides = along(sides, near)
     flow = kernel_call(
-        functools.partial(lower_kernel, early, rows, half, 4, nx), floats(2 * rows, PATCH),
-        later, above, other, rest, cross, flow, *constants,
-        scratch=region_scratch(late, half) + [half_of(late)] + stats_scratch(late, half),
+        functools.partial(shared_kernel, rows, half, 4, ny, nx), floats(2 * rows, PATCH),
+        tile, frame, rest, even, odd, sides, *tables(),
+        scratch=region_scratch(rows, half) + [pltpu.VMEM(half_shape(rows, half), jnp.float32)] * 2
+        + stats_scratch(rows, half),
     )
     window = kernel_call(
         functools.partial(window_kernel, half, nx), floats(*flow.shape),

time: 39.7 us -> 38.6 us (0.972)
  starting transfers between devices: 16.1 us -> 15.6 us
    ppermute x2, starting transfers between devices: 2.6 us -> 3.88 us  [pairs_odd(): lax.ppermute(value, 'ty', [(i, (i - 1 if i % 2 == 0 else i + 1) % size) f...]
    ppermute x2, starting transfers between devices: 1.2 us -> 0.05 us  [pairs_even(): return lax.ppermute(value, 'ty', [(i, i ^ 1) for i in range(size)])]
    ppermute x8 -> x6, waiting for transfers between devices: 10.5 us -> 9.59 us  [along(): return lax.ppermute(value, AXES, pairs)]
    ppermute x2, waiting for transfers between devices: 3.35 us -> 4.04 us  [pairs_odd(): lax.ppermute(value, 'ty', [(i, (i - 1 if i % 2 == 0 else i + 1) % size) f...]
    ppermute x8 -> x6, starting transfers between devices: 12.3 us -> 11.7 us  [along(): return lax.ppermute(value, AXES, pairs)]
  transfers between devices with their start and end apart: 12 -> 10, of which waited for: 6 -> 6; matrix products, arithmetic and copies ran while one was open for 0% -> 0% of each run, Pallas kernels for 10% -> 1%
where the time goes in v1:
time: 38.6 us; the launch traced here: 38.5 us
  starting transfers between devices  15.6 us (40%)
  waiting for transfers between devices  13.6 us (35%)
  Pallas kernels  7.49 us (19%)
  local copies, waits for them, and re-layouts  1.06 us (3%)
  between operations  0.71 us (2%)
    ppermute x6, starting transfers between devices, along(): return lax.ppermute(value, AXES, pairs)  11.7 us
    ppermute x6, waiting for transfers between devices, along(): return lax.ppermute(value, AXES, pairs)  9.59 us
    pallas_call x6, Pallas kernels, kernel_call(): pl.pallas_call(body, out_shape=shapes, in_specs=[IN_VMEM] * len(args), ou...  7.49 us
    ppermute x2, waiting for transfers between devices, pairs_odd(): lax.ppermute(value, 'ty', [(i, (i - 1 if i % 2 == 0 else i + 1) % size) f...  4.04 us
    ppermute x2, starting transfers between devices, pairs_odd(): lax.ppermute(value, 'ty', [(i, (i - 1 if i % 2 == 0 else i + 1) % size) f...  3.88 us
    unnamed x8, local copies, waits for them, and re-layouts  1.06 us
  transfers between devices with their start and end apart: 10, of which 6 were waited for; matrix products, arithmetic and copies ran while one was open for 0% of the time, Pallas kernels for 1%

profile of v1, /device:TPU:0, one launch (start us, length us, event | category | flops | bytes accessed | tf_op | source)
XLA Modules:
  0.0 38.5 jit_solution(11919894843760234166)
XLA Ops:
  0.6 0.0 copy-start
  0.6 1.0 %copy-done = f32[1,256,512]{2,1,0:T(8,128)S(1)} copy-done((f32[1,256,512]{2,1,0:T(8,128)S(1)}, f32[1,256,512]{2,1,0:T(8,128)}, u32[]{:S(2)}) %copy-start) | copy-done | bytes 524312
  1.7 0.2 shard_map.59
  1.9 3.0 %collective-permute-start = (f32[192,128]{1,0:T(8,128)S(1)}, f32[192,128]{1,0:T(8,128)S(1)}, u32[]{:S(2)}, u32[]{:S(2)}) collective-permute-start(f32[192,128]{1,0:T(8,128)S(1)} %get-tuple-element.6), channel_id=1, source_target_pairs={{0,16},{16,0},{17,1},{1,17},{2,18},{18,2},{19,3},{3,19},{4,20},{20... | collective-permute-start | bytes 294920 | tf_op jit(solution)/shard_map/ppermute | solution.py:250
  4.9 0.1 collective-permute-start.1
  5.0 3.4 %collective-permute-done.frame_ref = f32[192,128]{1,0:T(8,128)S(1)} collective-permute-done((f32[192,128]{1,0:T(8,128)S(1)}, f32[192,128]{1,0:T(8,128)S(1)}, u32[]{:S(2)}, u32[]{:S(2)}) %collective-permute-start) | collective-permute-done | bytes 98336 | tf_op jit(solution)/shard_map/ppermute | solution.py:250
  8.3 0.1 shard_map.60
  8.5 0.0 collective-permute-start.2
  8.5 0.0 copy-start.1
  8.5 0.0 copy-start.2
  8.5 0.0 copy-start.3
  8.6 2.3 %collective-permute-start.3 = (f32[144,128]{1,0:T(8,128)S(1)}, f32[144,128]{1,0:T(8,128)S(1)}, u32[]{:S(2)}, u32[]{:S(2)}) collective-permute-start(f32[144,128]{1,0:T(8,128)S(1)} %get-tuple-element.9), channel_id=1, source_target_pairs={{0,12},{4,8},{8,4},{12,0},{1,13},{5,9},{9,5},{13,1},{2,14},{6,10},... | collective-permute-start | bytes 221192 | tf_op jit(solution)/shard_map/ppermute | solution.py:272
  10.9 0.0 collective-permute-done.2.even_ref
  10.9 2.5 %collective-permute-done.3.odd_ref = f32[144,128]{1,0:T(8,128)S(1)} collective-permute-done((f32[144,128]{1,0:T(8,128)S(1)}, f32[144,128]{1,0:T(8,128)S(1)}, u32[]{:S(2)}, u32[]{:S(2)}) %collective-permute-start.3) | collective-permute-done | bytes 73760 | tf_op jit(solution)/shard_map/ppermute | solution.py:272
  13.4 0.2 shard_map.61
  13.6 3.7 %collective-permute-start.4 = (f32[160,128]{1,0:T(8,128)S(1)}, f32[160,128]{1,0:T(8,128)S(1)}, u32[]{:S(2)}, u32[]{:S(2)}) collective-permute-start(f32[160,128]{1,0:T(8,128)S(1)} %shard_map.61), channel_id=1, source_target_pairs={{0,3},{16,17},{17,16},{1,2},{2,1},{18,19},{19,18},{3,0},{4,7},{20,... | collective-permute-start | bytes 245768 | tf_op jit(solution)/shard_map/ppermute | solution.py:250
  17.4 0.0 collective-permute-done.1.rest_ref
  17.4 3.1 %collective-permute-done.4.sides_ref = f32[160,128]{1,0:T(8,128)S(1)} collective-permute-done((f32[160,128]{1,0:T(8,128)S(1)}, f32[160,128]{1,0:T(8,128)S(1)}, u32[]{:S(2)}, u32[]{:S(2)}) %collective-permute-start.4) | collective-permute-done | bytes 81952 | tf_op jit(solution)/shard_map/ppermute | solution.py:250
  20.5 0.0 copy-done.1
  20.5 0.0 copy-done.2
  20.5 0.0 copy-done.3
  20.5 6.0 %shard_map.62.own_ref = f32[8,128]{1,0:T(8,128)S(1)} custom-call(f32[256,512]{1,0:T(8,128)S(1)} %bitcast.4, f32[192,128]{1,0:T(8,128)S(1)} %collective-permute-done.frame_ref, f32[192,256]{1,0:T(8,128)S(1)} %collective-permute-done.1.rest_ref, f32[144,128]{1,0:T(8,128)S(1)} %collective-permute-done.2.even_ref, ...), custom_call_target="tpu_custom_call" | custom-call | tf_op jit(solution)/shard_map/pallas_call | solution.py:160
  26.5 0.0 collective-permute-start.5
  26.5 3.4 %collective-permute-start.6 = (f32[8,128]{1,0:T(8,128)S(1)}, f32[8,128]{1,0:T(8,128)S(1)}, u32[]{:S(2)}, u32[]{:S(2)}) collective-permute-start(f32[8,128]{1,0:T(8,128)S(1)} %shard_map.62.own_ref), channel_id=1, source_target_pairs={{0,3},{16,17},{17,16},{1,2},{2,1},{18,19},{19,18},{3,0},{4,7},{20,... | collective-permute-start | bytes 12296 | tf_op jit(solution)/shard_map/ppermute | solution.py:250
  29.9 1.4 %collective-permute-start.7 = (f32[8,128]{1,0:T(8,128)S(1)}, f32[8,128]{1,0:T(8,128)S(1)}, u32[]{:S(2)}, u32[]{:S(2)}) collective-permute-start(f32[8,128]{1,0:T(8,128)S(1)} %shard_map.62.own_ref), channel_id=1, source_target_pairs={{0,19},{16,1},{17,0},{1,18},{2,17},{18,3},{19,2},{3,16},{4,23},{20... | collective-permute-start | bytes 12296 | tf_op jit(solution)/shard_map/ppermute | solution.py:250
  31.3 0.0 collective-permute-done.5.mate_ref
  31.3 0.7 %collective-permute-done.6.near_ref = f32[8,128]{1,0:T(8,128)S(1)} collective-permute-done((f32[8,128]{1,0:T(8,128)S(1)}, f32[8,128]{1,0:T(8,128)S(1)}, u32[]{:S(2)}, u32[]{:S(2)}) %collective-permute-start.6) | collective-permute-done | bytes 4128 | tf_op jit(solution)/shard_map/ppermute | solution.py:250
  32.0 2.4 %collective-permute-done.7.far_ref = f32[8,128]{1,0:T(8,128)S(1)} collective-permute-done((f32[8,128]{1,0:T(8,128)S(1)}, f32[8,128]{1,0:T(8,128)S(1)}, u32[]{:S(2)}, u32[]{:S(2)}) %collective-permute-start.7) | collective-permute-done | bytes 4128 | tf_op jit(solution)/shard_map/ppermute | solution.py:250
  34.5 0.1 shard_map.63.own_ref
  34.5 0.0 collective-permute-start.8
  34.6 1.6 %collective-permute-start.9 = (f32[8,128]{1,0:T(8,128)S(1)}, f32[8,128]{1,0:T(8,128)S(1)}, u32[]{:S(2)}, u32[]{:S(2)}) collective-permute-start(f32[8,128]{1,0:T(8,128)S(1)} %shard_map.63.own_ref), channel_id=1, source_target_pairs={{0,12},{4,8},{8,4},{12,0},{1,13},{5,9},{9,5},{13,1},{2,14},{6,10},... | collective-permute-start | bytes 12296 | tf_op jit(solution)/shard_map/ppermute | solution.py:272
  36.1 0.0 collective-permute-done.8.even_ref
  36.1 1.5 %collective-permute-done.9.odd_ref = f32[8,128]{1,0:T(8,128)S(1)} collective-permute-done((f32[8,128]{1,0:T(8,128)S(1)}, f32[8,128]{1,0:T(8,128)S(1)}, u32[]{:S(2)}, u32[]{:S(2)}) %collective-permute-start.9) | collective-permute-done | bytes 4128 | tf_op jit(solution)/shard_map/ppermute | solution.py:272
  37.7 0.8 %shard_map.64 = (f32[1,2,4,8]{3,2,1,0:T(4,128)}, f32[1,2,4,8]{3,2,1,0:T(4,128)}) custom-call(f32[8,128]{1,0:T(8,128)S(1)} %shard_map.63.own_ref, f32[8,128]{1,0:T(8,128)S(1)} %collective-permute-done.8.even_ref, f32[8,128]{1,0:T(8,128)S(1)} %collective-permute-done.9.odd_ref), custom_call_target="tpu_custom_call" | custom-call | tf_op jit(solution)/shard_map/pallas_call | solution.py:160
Async XLA Ops:
  0.6 1.0 %copy-start = (f32[1,256,512]{2,1,0:T(8,128)S(1)}, f32[1,256,512]{2,1,0:T(8,128)}, u32[]{:S(2)}) copy-start(f32[1,256,512]{2,1,0:T(8,128)} %param.4) | copy-start | bytes 1572868
  1.9 6.4 %collective-permute-start = (f32[192,128]{1,0:T(8,128)S(1)}, f32[192,128]{1,0:T(8,128)S(1)}, u32[]{:S(2)}, u32[]{:S(2)}) collective-permute-start(f32[192,128]{1,0:T(8,128)S(1)} %get-tuple-element.6), channel_id=1, source_target_pairs={{0,16},{16,0},{17,1},{1,17},{2,18},{18,2},{19,3},{3,19},{4,20},{20... | collective-permute-start | bytes 294920 | tf_op jit(solution)/shard_map/ppermute | solution.py:250
  4.9 12.5 %collective-permute-start.1 = (f32[192,256]{1,0:T(8,128)S(1)}, f32[192,256]{1,0:T(8,128)S(1)}, u32[]{:S(2)}, u32[]{:S(2)}) collective-permute-start(f32[192,256]{1,0:T(8,128)S(1)} %get-tuple-element.7), channel_id=1, source_target_pairs={{0,16},{16,0},{17,1},{1,17},{2,18},{18,2},{19,3},{3,19},{4,20},{20... | collective-permute-start | bytes 589832 | tf_op jit(solution)/shard_map/ppermute | solution.py:250
  8.5 2.4 %collective-permute-start.2 = (f32[144,128]{1,0:T(8,128)S(1)}, f32[144,128]{1,0:T(8,128)S(1)}, u32[]{:S(2)}, u32[]{:S(2)}) collective-permute-start(f32[144,128]{1,0:T(8,128)S(1)} %get-tuple-element.8), channel_id=1, source_target_pairs={{0,4},{4,0},{8,12},{12,8},{1,5},{5,1},{9,13},{13,9},{2,6},{6,2},{1... | collective-permute-start | bytes 221192 | tf_op jit(solution)/shard_map/ppermute | solution.py:267
  8.5 11.9 %copy-start.1 = (bf16[2,256,256]{2,1,0:T(8,128)(2,1)S(1)}, bf16[2,256,256]{2,1,0:T(8,128)(2,1)}, u32[]{:S(2)}) copy-start(bf16[2,256,256]{2,1,0:T(8,128)(2,1)} %constant.7.clone.right_ref) | copy-start | bytes 786436
  8.5 11.9 %copy-start.2 = (bf16[128,432]{1,0:T(8,128)(2,1)S(1)}, bf16[128,432]{1,0:T(8,128)(2,1)}, u32[]{:S(2)}) copy-start(bf16[128,432]{1,0:T(8,128)(2,1)} %constant.8.clone.back_ref) | copy-start | bytes 331780
  8.5 11.9 %copy-start.3 = (bf16[144,384]{1,0:T(8,128)(2,1)S(1)}, bf16[144,384]{1,0:T(8,128)(2,1)}, u32[]{:S(2)}) copy-start(bf16[144,384]{1,0:T(8,128)(2,1)} %constant.6.clone.left_ref) | copy-start | bytes 331780
  8.6 4.8 %collective-permute-start.3 = (f32[144,128]{1,0:T(8,128)S(1)}, f32[144,128]{1,0:T(8,128)S(1)}, u32[]{:S(2)}, u32[]{:S(2)}) collective-permute-start(f32[144,128]{1,0:T(8,128)S(1)} %get-tuple-element.9), channel_id=1, source_target_pairs={{0,12},{4,8},{8,4},{12,0},{1,13},{5,9},{9,5},{13,1},{2,14},{6,10},... | collective-permute-start | bytes 221192 | tf_op jit(solution)/shard_map/ppermute | solution.py:272
  13.6 6.9 %collective-permute-start.4 = (f32[160,128]{1,0:T(8,128)S(1)}, f32[160,128]{1,0:T(8,128)S(1)}, u32[]{:S(2)}, u32[]{:S(2)}) collective-permute-start(f32[160,128]{1,0:T(8,128)S(1)} %shard_map.61), channel_id=1, source_target_pairs={{0,3},{16,17},{17,16},{1,2},{2,1},{18,19},{19,18},{3,0},{4,7},{20,... | collective-permute-start | bytes 245768 | tf_op jit(solution)/shard_map/ppermute | solution.py:250
  26.5 4.9 %collective-permute-start.5 = (f32[8,128]{1,0:T(8,128)S(1)}, f32[8,128]{1,0:T(8,128)S(1)}, u32[]{:S(2)}, u32[]{:S(2)}) collective-permute-start(f32[8,128]{1,0:T(8,128)S(1)} %shard_map.62.own_ref), channel_id=1, source_target_pairs={{0,16},{16,0},{17,1},{1,17},{2,18},{18,2},{19,3},{3,19},{4,20},{20... | collective-permute-start | bytes 12296 | tf_op jit(solution)/shard_map/ppermute | solution.py:250
  26.5 5.5 %collective-permute-start.6 = (f32[8,128]{1,0:T(8,128)S(1)}, f32[8,128]{1,0:T(8,128)S(1)}, u32[]{:S(2)}, u32[]{:S(2)}) collective-permute-start(f32[8,128]{1,0:T(8,128)S(1)} %shard_map.62.own_ref), channel_id=1, source_target_pairs={{0,3},{16,17},{17,16},{1,2},{2,1},{18,19},{19,18},{3,0},{4,7},{20,... | collective-permute-start | bytes 12296 | tf_op jit(solution)/shard_map/ppermute | solution.py:250
  29.9 4.5 %collective-permute-start.7 = (f32[8,128]{1,0:T(8,128)S(1)}, f32[8,128]{1,0:T(8,128)S(1)}, u32[]{:S(2)}, u32[]{:S(2)}) collective-permute-start(f32[8,128]{1,0:T(8,128)S(1)} %shard_map.62.own_ref), channel_id=1, source_target_pairs={{0,19},{16,1},{17,0},{1,18},{2,17},{18,3},{19,2},{3,16},{4,23},{20... | collective-permute-start | bytes 12296 | tf_op jit(solution)/shard_map/ppermute | solution.py:250
  34.5 1.6 %collective-permute-start.8 = (f32[8,128]{1,0:T(8,128)S(1)}, f32[8,128]{1,0:T(8,128)S(1)}, u32[]{:S(2)}, u32[]{:S(2)}) collective-permute-start(f32[8,128]{1,0:T(8,128)S(1)} %shard_map.63.own_ref), channel_id=1, source_target_pairs={{0,4},{4,0},{8,12},{12,8},{1,5},{5,1},{9,13},{13,9},{2,6},{6,2},{1... | collective-permute-start | bytes 12296 | tf_op jit(solution)/shard_map/ppermute | solution.py:267
  34.6 3.1 %collective-permute-start.9 = (f32[8,128]{1,0:T(8,128)S(1)}, f32[8,128]{1,0:T(8,128)S(1)}, u32[]{:S(2)}, u32[]{:S(2)}) collective-permute-start(f32[8,128]{1,0:T(8,128)S(1)} %shard_map.63.own_ref), channel_id=1, source_target_pairs={{0,12},{4,8},{8,4},{12,0},{1,13},{5,9},{9,5},{13,1},{2,14},{6,10},... | collective-permute-start | bytes 12296 | tf_op jit(solution)/shard_map/ppermute | solution.py:272

commit v2 on v1

--- a/solution.py
+++ b/solution.py
@@ -262,6 +262,10 @@
     return g - 2 if g % 2 == 0 else g + 2
 
 
+def past(g):
+    return g + 2 if g % 2 == 0 else g - 2
+
+
 def pairs_even(value):
     size = lax.axis_size("ty")
     return lax.ppermute(value, "ty", [(i, i ^ 1) for i in range(size)])
@@ -309,114 +313,82 @@
     return slice(0, core) if half == 0 else slice(width - core, width)
 
 
-def edge_of(half, value):
-    return value[:, :HALF] if half == 0 else value[:, value.shape[1] - HALF:]
-
-
-def body_of(half, value):
-    return value[:, HALF:] if half == 0 else value[:, :value.shape[1] - HALF]
-
-
 def by_half(half, branch):
     for h in range(2):
         pl.when(half == h)(functools.partial(branch, h))
 
 
-def cut_kernel(core, tile_ref, frame_ref, rest_ref):
-    _, _, _, half = where_am_i()
-    tall, width = tile_ref.shape
-
-    def branch(h):
-        value = tile_ref[:, own_lanes(1 - h, core, width)]
-        middle = value[HALF:tall - HALF]
-        ends = jnp.concatenate([value[:HALF], value[tall - HALF:]], axis=0)
-        frame_ref[...] = jnp.concatenate([packed_wide(ends), packed(edge_of(1 - h, middle))], axis=0)
-        rest_ref[...] = body_of(1 - h, middle)
-
-    by_half(half, branch)
-
-
-def ends_of(core, frame):
-    return unpacked_wide(frame, 2 * HALF, core)
-
-
-def side_of(tall, frame):
-    return unpacked(frame[frame.shape[0] - (tall - 2 * HALF) // 4:])
-
-
-def strips_kernel(core, tile_ref, frame_ref, even_ref, odd_ref):
+def cut_kernel(core, tile_ref, other_ref, even_ref, odd_ref):
     _, y, _, half = where_am_i()
     tall, width = tile_ref.shape
     lower = y % 2 == 1
-    ends = ends_of(core, frame_ref[...])
+    first, last = tile_ref[:HALF], tile_ref[tall - HALF:]
+    even_ref[...] = jnp.where(lower, first, last)
+    odd_ref[...] = jnp.where(lower, last, first)
 
     def branch(h):
+        other_ref[...] = packed_wide(tile_ref[:, own_lanes(1 - h, core, width)])
+
+    by_half(half, branch)
+
+
+def borders_kernel(core, ny, tile_ref, even_ref, odd_ref, strips_ref, near_ref, past_ref):
+    _, y, _, half = where_am_i()
+    width = tile_ref.shape[1]
+    above, below = around(y, ny, even_ref[...], odd_ref[...])
+
+    def column(lanes):
+        return packed(jnp.concatenate([above[:, lanes], tile_ref[:, lanes], below[:, lanes]], axis=0))
+
+    first, last = column(slice(0, HALF)), column(slice(width - HALF, width))
+
+    def branch(h):
+        lanes = own_lanes(1 - h, core, width)
+        strips_ref[...] = packed_wide(jnp.concatenate([above[:, lanes], below[:, lanes]], axis=0))
+        near_ref[...], past_ref[...] = (first, last) if h == 0 else (last, first)
+
+    by_half(half, branch)
+
+
+def keep_half(half, x, nx, cols, side_ref, values, high_ref, low_ref):
+    at_end = jnp.where(half == 0, x == 0, x == nx - 1)
+    side = jnp.where(at_end, 0.0, unpacked(side_ref[...]))
+
+    def branch(h):
+        value = jnp.concatenate([side, values(h)] if h == 0 else [values(h), side], axis=1)
+        keep_region(value, cols * STRIDE, high_ref, low_ref)
+
+    by_half(half, branch)
+
+
+def own_kernel(rows, cols, ny, nx, tile_ref, even_ref, odd_ref, side_ref, left_ref, half_ref, high_ref, low_ref):
+    _, y, x, half = where_am_i()
+    width, core = tile_ref.shape[1], cols * STRIDE + HALF
+    above, below = around(y, ny, even_ref[...], odd_ref[...])
+
+    def values(h):
         lanes = own_lanes(h, core, width)
-        first = packed_wide(jnp.concatenate([tile_ref[:HALF, lanes], ends[:HALF]], axis=0))
-        last = packed_wide(jnp.concatenate([tile_ref[tall - HALF:, lanes], ends[HALF:]], axis=0))
-        even_ref[...] = jnp.where(lower, first, last)
-        odd_ref[...] = jnp.where(lower, last, first)
-
-    by_half(half, branch)
-
-
-def strips_of(core, y, ny, even_ref, odd_ref):
-    above, below = around(y, ny, even_ref[...], odd_ref[...])
-    return unpacked_wide(above, 2 * HALF, core), unpacked_wide(below, 2 * HALF, core)
-
-
-def sides_kernel(core, ny, tile_ref, frame_ref, even_ref, odd_ref, side_ref):
-    _, y, _, half = where_am_i()
-    tall, width = tile_ref.shape
-    above, below = strips_of(core, y, ny, even_ref, odd_ref)
-    ends, side = ends_of(core, frame_ref[...]), side_of(tall, frame_ref[...])
-
-    def branch(h):
-        own = edge_of(h, tile_ref[:, own_lanes(h, core, width)])
-        over, under = edge_of(h, above), edge_of(h, below)
-        limits = edge_of(h, ends)
-        side_ref[...] = jnp.concatenate(
-            [packed(jnp.concatenate([over[:HALF], own, under[:HALF]], axis=0)),
-             packed(jnp.concatenate([over[HALF:], limits[:HALF], side, limits[HALF:], under[HALF:]], axis=0))],
-            axis=0)
-
-    by_half(half, branch)
-
-
-def shared_kernel(rows, cols, group, ny, nx, tile_ref, frame_ref, rest_ref, even_ref, odd_ref, sides_ref,
-                  left_ref, right_ref, back_ref, flow_ref, high_ref, low_ref, own_half, other_half, *stats):
-    section, y, x, half = where_am_i()
-    tall, width = tile_ref.shape
+        return jnp.concatenate([above[:, lanes], tile_ref[:, lanes], below[:, lanes]], axis=0)
+
+    keep_half(half, x, nx, cols, side_ref, values, high_ref, low_ref)
+    left_dft(cols, range(rows), high_ref, low_ref, left_ref, half_ref)
+
+
+def pair_kernel(rows, cols, group, nx, own_ref, other_ref, strips_ref, cross_ref,
+                left_ref, right_ref, back_ref, flow_ref, high_ref, low_ref, half_ref, *stats):
+    section, _, x, half = where_am_i()
     core = cols * STRIDE + HALF
-    above, below = strips_of(core, y, ny, even_ref, odd_ref)
-    ends, side = ends_of(core, frame_ref[...]), side_of(tall, frame_ref[...])
-    at_end = jnp.where(half == 0, x == 0, x == nx - 1)
-    sides = jnp.where(at_end, 0.0, sides_ref[...])
-    quarter = sides.shape[0] // 2
-    own_side, other_side = unpacked(sides[:quarter]), unpacked(sides[quarter:])
-
-    def joined(h, outer, value):
-        return jnp.concatenate([outer, value] if h == 0 else [value, outer], axis=1)
-
-    def own_branch(h):
-        middle = tile_ref[:, own_lanes(h, core, width)]
-        value = jnp.concatenate([above[:HALF], middle, below[:HALF]], axis=0)
-        keep_region(joined(h, own_side, value), cols * STRIDE, high_ref, low_ref)
-
-    def other_branch(h):
-        middle = joined(h, side, rest_ref[...])
-        value = jnp.concatenate([above[HALF:], ends[:HALF], middle, ends[HALF:], below[HALF:]], axis=0)
-        keep_region(joined(h, other_side, value), cols * STRIDE, high_ref, low_ref)
-
-    for branch, half_ref in ((own_branch, own_half), (other_branch, other_half)):
-        by_half(half, branch)
-        left_dft(cols, range(rows), high_ref, low_ref, left_ref, half_ref)
+    strips = unpacked_wide(strips_ref[...], 2 * HALF, core)
+    middle = unpacked_wide(other_ref[...], rows * STRIDE, core)
+    value = jnp.concatenate([strips[:HALF], middle, strips[HALF:]], axis=0)
+    keep_half(half, x, nx, cols, cross_ref, lambda h: value, high_ref, low_ref)
+    left_dft(cols, range(rows), high_ref, low_ref, left_ref, half_ref)
 
     def put(c, i, row):
         flow_ref[c * rows + i:c * rows + i + 1, :] = row
 
     sign = jnp.where(section == 0, 1.0, -1.0)
-    correlate(rows, cols, group, sign, own_half, other_half, right_ref, back_ref, put, *stats)
+    correlate(rows, cols, group, sign, own_ref, half_ref, right_ref, back_ref, put, *stats)
 
 
 def window_kernel(width, nx, own_ref, mate_ref, near_ref, far_ref, out_ref):
@@ -471,25 +443,29 @@
     half = cols // 2
     core, tall = half * STRIDE + HALF, tile.shape[0]
 
-    wide = 2 * HALF * core // PATCH
-    strip = floats(wide, PATCH)
-    frame, rest = kernel_call(
-        functools.partial(cut_kernel, core),
-        (floats(wide + (tall - 2 * HALF) // 4, PATCH), floats(tall - 2 * HALF, core - HALF)), tile,
-    )
-    frame, rest = along(frame, mate), along(rest, mate)
-    even, odd = kernel_call(functools.partial(strips_kernel, core), (strip, strip), tile, frame)
+    strip = floats(HALF, tile.shape[1])
+    other, even, odd = kernel_call(
+        functools.partial(cut_kernel, core), (floats(tall * core // PATCH, PATCH), strip, strip), tile,
+    )
+    other = along(other, mate)
     even, odd = pairs_even(even), pairs_odd(odd)
-    sides = kernel_call(
-        functools.partial(sides_kernel, core, ny), floats((tall + 2 * HALF) // 2, PATCH),
-        tile, frame, even, odd,
-    )
-    sides = along(sides, near)
+    edge = floats((tall + 2 * HALF) // 4, PATCH)
+    strips, side, cross = kernel_call(
+        functools.partial(borders_kernel, core, ny), (floats(2 * HALF * core // PATCH, PATCH), edge, edge),
+        tile, even, odd,
+    )
+    side, cross = along(side, near), along(cross, past)
+    strips = along(strips, mate)
+    left, right, back = tables()
+    spectra = half_shape(rows, half)
+    own = kernel_call(
+        functools.partial(own_kernel, rows, half, ny, nx), floats(*spectra), tile, even, odd, side, left,
+        scratch=region_scratch(rows, half),
+    )
     flow = kernel_call(
-        functools.partial(shared_kernel, rows, half, 4, ny, nx), floats(2 * rows, PATCH),
-        tile, frame, rest, even, odd, sides, *tables(),
-        scratch=region_scratch(rows, half) + [pltpu.VMEM(half_shape(rows, half), jnp.float32)] * 2
-        + stats_scratch(rows, half),
+        functools.partial(pair_kernel, rows, half, 4, nx), floats(2 * rows, PATCH),
+        own, other, strips, cross, left, right, back,
+        scratch=region_scratch(rows, half) + [pltpu.VMEM(spectra, jnp.float32)] + stats_scratch(rows, half),
     )
     window = kernel_call(
         functools.partial(window_kernel, half, nx), floats(*flow.shape),

time: 38.6 us -> 34.8 us (0.902)
  waiting for transfers between devices: 13.6 us -> 11.6 us
  starting transfers between devices: 15.6 us -> 13.8 us
    ppermute x2, starting transfers between devices: 3.88 us -> 1.62 us  [pairs_odd(): lax.ppermute(value, 'ty', [(i, (i - 1 if i % 2 == 0 else i + 1) % size) f...]
    ppermute x2, starting transfers between devices: 0.05 us -> 1.59 us  [pairs_even(): return lax.ppermute(value, 'ty', [(i, i ^ 1) for i in range(size)])]
    ppermute x6 -> x7, waiting for transfers between devices: 9.59 us -> 8.11 us  [along(): return lax.ppermute(value, AXES, pairs)]
    ppermute x6 -> x7, starting transfers between devices: 11.7 us -> 10.6 us  [along(): return lax.ppermute(value, AXES, pairs)]
    ppermute x2, waiting for transfers between devices: 4.04 us -> 3.52 us  [pairs_odd(): lax.ppermute(value, 'ty', [(i, (i - 1 if i % 2 == 0 else i + 1) % size) f...]
  transfers between devices with their start and end apart: 10 -> 11, of which waited for: 6 -> 6; matrix products, arithmetic and copies ran while one was open for 0% -> 0% of each run, Pallas kernels for 1% -> 3%
where the time goes in v2:
time: 34.8 us; the launch traced here: 34.6 us
  starting transfers between devices  13.8 us (40%)
  waiting for transfers between devices  11.6 us (33%)
  Pallas kernels  7.42 us (21%)
  local copies, waits for them, and re-layouts  1.05 us (3%)
  between operations  0.69 us (2%)
    ppermute x7, starting transfers between devices, along(): return lax.ppermute(value, AXES, pairs)  10.6 us
    ppermute x7, waiting for transfers between devices, along(): return lax.ppermute(value, AXES, pairs)  8.11 us
    pallas_call x6, Pallas kernels, kernel_call(): pl.pallas_call(body, out_shape=shapes, in_specs=[IN_VMEM] * len(args), ou...  7.42 us
    ppermute x2, waiting for transfers between devices, pairs_odd(): lax.ppermute(value, 'ty', [(i, (i - 1 if i % 2 == 0 else i + 1) % size) f...  3.52 us
    ppermute x2, starting transfers between devices, pairs_odd(): lax.ppermute(value, 'ty', [(i, (i - 1 if i % 2 == 0 else i + 1) % size) f...  1.62 us
    ppermute x2, starting transfers between devices, pairs_even(): return lax.ppermute(value, 'ty', [(i, i ^ 1) for i in range(size)])  1.59 us
    unnamed x8, local copies, waits for them, and re-layouts  1.05 us
  transfers between devices with their start and end apart: 11, of which 6 were waited for; matrix products, arithmetic and copies ran while one was open for 0% of the time, Pallas kernels for 3%

profile of v2, /device:TPU:0, one launch (start us, length us, event | category | flops | bytes accessed | tf_op | source)
XLA Modules:
  0.0 34.6 jit_solution(14809587226024859566)
XLA Ops:
  0.6 0.0 copy-start
  0.6 1.0 %copy-done = f32[1,256,512]{2,1,0:T(8,128)S(1)} copy-done((f32[1,256,512]{2,1,0:T(8,128)S(1)}, f32[1,256,512]{2,1,0:T(8,128)}, u32[]{:S(2)}) %copy-start) | copy-done | bytes 524312
  1.7 0.0 copy-start.1
  1.7 0.2 shard_map.59
  1.9 2.9 %collective-permute-start.3 = (f32[576,128]{1,0:T(8,128)S(1)}, f32[576,128]{1,0:T(8,128)S(1)}, u32[]{:S(2)}, u32[]{:S(2)}) collective-permute-start(f32[576,128]{1,0:T(8,128)S(1)} %get-tuple-element.11), channel_id=1, source_target_pairs={{0,16},{16,0},{17,1},{1,17},{2,18},{18,2},{19,3},{3,19},{4,20},{20... | collective-permute-start | bytes 884744 | tf_op jit(solution)/shard_map/ppermute | solution.py:250
  4.9 0.0 collective-permute-start
  4.9 0.0 copy-start.2
  4.9 0.0 copy-start.3
  4.9 1.6 %collective-permute-start.1 = (f32[32,512]{1,0:T(8,128)S(1)}, f32[32,512]{1,0:T(8,128)S(1)}, u32[]{:S(2)}, u32[]{:S(2)}) collective-permute-start(f32[32,512]{1,0:T(8,128)S(1)} %get-tuple-element.9), channel_id=1, source_target_pairs={{0,12},{4,8},{8,4},{12,0},{1,13},{5,9},{9,5},{13,1},{2,14},{6,10},... | collective-permute-start | bytes 196616 | tf_op jit(solution)/shard_map/ppermute | solution.py:276
  6.5 0.0 collective-permute-done.even_ref
  6.5 2.1 %collective-permute-done.1.odd_ref = f32[32,512]{1,0:T(8,128)S(1)} collective-permute-done((f32[32,512]{1,0:T(8,128)S(1)}, f32[32,512]{1,0:T(8,128)S(1)}, u32[]{:S(2)}, u32[]{:S(2)}) %collective-permute-start.1) | collective-permute-done | bytes 65568 | tf_op jit(solution)/shard_map/ppermute | solution.py:276
  8.6 0.3 shard_map.60
  8.8 0.9 %collective-permute-start.4 = (f32[144,128]{1,0:T(8,128)S(1)}, f32[144,128]{1,0:T(8,128)S(1)}, u32[]{:S(2)}, u32[]{:S(2)}) collective-permute-start(f32[144,128]{1,0:T(8,128)S(1)} %get-tuple-element.12), channel_id=1, source_target_pairs={{0,16},{16,0},{17,1},{1,17},{2,18},{18,2},{19,3},{3,19},{4,20},{20... | collective-permute-start | bytes 221192 | tf_op jit(solution)/shard_map/ppermute | solution.py:250
  9.7 3.3 %collective-permute-start.2 = (f32[80,128]{1,0:T(8,128)S(1)}, f32[80,128]{1,0:T(8,128)S(1)}, u32[]{:S(2)}, u32[]{:S(2)}) collective-permute-start(f32[80,128]{1,0:T(8,128)S(1)} %get-tuple-element.10), channel_id=1, source_target_pairs={{0,3},{16,17},{17,16},{1,2},{2,1},{18,19},{19,18},{3,0},{4,7},{20,... | collective-permute-start | bytes 122888 | tf_op jit(solution)/shard_map/ppermute | solution.py:250
  13.0 0.0 collective-permute-start.5
  13.0 2.5 %collective-permute-done.2.side_ref = f32[80,128]{1,0:T(8,128)S(1)} collective-permute-done((f32[80,128]{1,0:T(8,128)S(1)}, f32[80,128]{1,0:T(8,128)S(1)}, u32[]{:S(2)}, u32[]{:S(2)}) %collective-permute-start.2) | collective-permute-done | bytes 40992 | tf_op jit(solution)/shard_map/ppermute | solution.py:250
  15.5 0.0 copy-done.1
  15.5 0.9 %shard_map.61.own_ref = f32[16,72,256]{2,1,0:T(8,128)S(1)} custom-call(f32[256,512]{1,0:T(8,128)S(1)} %bitcast.3, f32[32,512]{1,0:T(8,128)S(1)} %collective-permute-done.even_ref, f32[32,512]{1,0:T(8,128)S(1)} %collective-permute-done.1.odd_ref, f32[80,128]{1,0:T(8,128)S(1)} %collective-permute-done.2.side_ref, bf16[144,384]{1,0:T(8,128)(2,1)S(1)} %copy-done.1), custom_call_target="tpu_custom_call" | custom-call | tf_op jit(solution)/shard_map/pallas_call | solution.py:160
  16.4 3.2 %collective-permute-done.5.cross_ref = f32[80,128]{1,0:T(8,128)S(1)} collective-permute-done((f32[80,128]{1,0:T(8,128)S(1)}, f32[80,128]{1,0:T(8,128)S(1)}, u32[]{:S(2)}, u32[]{:S(2)}) %collective-permute-start.5) | collective-permute-done | bytes 40992 | tf_op jit(solution)/shard_map/ppermute | solution.py:250
  19.7 0.0 collective-permute-done.4.strips_ref
  19.7 0.0 collective-permute-done.3.other_ref
  19.7 0.0 copy-done.2
  19.7 0.0 copy-done.3
  19.7 5.1 %shard_map.62.own_ref = f32[8,128]{1,0:T(8,128)S(1)} custom-call(f32[16,72,256]{2,1,0:T(8,128)S(1)} %shard_map.61.own_ref, f32[576,128]{1,0:T(8,128)S(1)} %collective-permute-done.3.other_ref, f32[144,128]{1,0:T(8,128)S(1)} %collective-permute-done.4.strips_ref, f32[80,128]{1,0:T(8,128)S(1)} %collective-permute-done.5.cross_ref, ...), custom_call_target="tpu_custom_call" | custom-call | tf_op jit(solution)/shard_map/pallas_call | solution.py:160
  24.8 0.5 %collective-permute-start.8 = (f32[8,128]{1,0:T(8,128)S(1)}, f32[8,128]{1,0:T(8,128)S(1)}, u32[]{:S(2)}, u32[]{:S(2)}) collective-permute-start(f32[8,128]{1,0:T(8,128)S(1)} %shard_map.62.own_ref), channel_id=1, source_target_pairs={{0,19},{16,1},{17,0},{1,18},{2,17},{18,3},{19,2},{3,16},{4,23},{20... | collective-permute-start | bytes 12296 | tf_op jit(solution)/shard_map/ppermute | solution.py:250
  25.2 0.7 %collective-permute-start.7 = (f32[8,128]{1,0:T(8,128)S(1)}, f32[8,128]{1,0:T(8,128)S(1)}, u32[]{:S(2)}, u32[]{:S(2)}) collective-permute-start(f32[8,128]{1,0:T(8,128)S(1)} %shard_map.62.own_ref), channel_id=1, source_target_pairs={{0,3},{16,17},{17,16},{1,2},{2,1},{18,19},{19,18},{3,0},{4,7},{20,... | collective-permute-start | bytes 12296 | tf_op jit(solution)/shard_map/ppermute | solution.py:250
  26.0 2.3 %collective-permute-start.6 = (f32[8,128]{1,0:T(8,128)S(1)}, f32[8,128]{1,0:T(8,128)S(1)}, u32[]{:S(2)}, u32[]{:S(2)}) collective-permute-start(f32[8,128]{1,0:T(8,128)S(1)} %shard_map.62.own_ref), channel_id=1, source_target_pairs={{0,16},{16,0},{17,1},{1,17},{2,18},{18,2},{19,3},{3,19},{4,20},{20... | collective-permute-start | bytes 12296 | tf_op jit(solution)/shard_map/ppermute | solution.py:250
  28.3 1.0 %collective-permute-done.8.far_ref = f32[8,128]{1,0:T(8,128)S(1)} collective-permute-done((f32[8,128]{1,0:T(8,128)S(1)}, f32[8,128]{1,0:T(8,128)S(1)}, u32[]{:S(2)}, u32[]{:S(2)}) %collective-permute-start.8) | collective-permute-done | bytes 4128 | tf_op jit(solution)/shard_map/ppermute | solution.py:250
  29.3 1.3 %collective-permute-done.7.near_ref = f32[8,128]{1,0:T(8,128)S(1)} collective-permute-done((f32[8,128]{1,0:T(8,128)S(1)}, f32[8,128]{1,0:T(8,128)S(1)}, u32[]{:S(2)}, u32[]{:S(2)}) %collective-permute-start.7) | collective-permute-done | bytes 4128 | tf_op jit(solution)/shard_map/ppermute | solution.py:250
  30.6 0.0 collective-permute-done.6.mate_ref
  30.6 0.1 shard_map.63.own_ref
  30.7 0.0 collective-permute-start.10
  30.7 1.6 %collective-permute-start.9 = (f32[8,128]{1,0:T(8,128)S(1)}, f32[8,128]{1,0:T(8,128)S(1)}, u32[]{:S(2)}, u32[]{:S(2)}) collective-permute-start(f32[8,128]{1,0:T(8,128)S(1)} %shard_map.63.own_ref), channel_id=1, source_target_pairs={{0,4},{4,0},{8,12},{12,8},{1,5},{5,1},{9,13},{13,9},{2,6},{6,2},{1... | collective-permute-start | bytes 12296 | tf_op jit(solution)/shard_map/ppermute | solution.py:271
  32.3 1.4 %collective-permute-done.10.odd_ref = f32[8,128]{1,0:T(8,128)S(1)} collective-permute-done((f32[8,128]{1,0:T(8,128)S(1)}, f32[8,128]{1,0:T(8,128)S(1)}, u32[]{:S(2)}, u32[]{:S(2)}) %collective-permute-start.10) | collective-permute-done | bytes 4128 | tf_op jit(solution)/shard_map/ppermute | solution.py:276
  33.8 0.0 collective-permute-done.9.even_ref
  33.8 0.8 %shard_map.64 = (f32[1,2,4,8]{3,2,1,0:T(4,128)}, f32[1,2,4,8]{3,2,1,0:T(4,128)}) custom-call(f32[8,128]{1,0:T(8,128)S(1)} %shard_map.63.own_ref, f32[8,128]{1,0:T(8,128)S(1)} %collective-permute-done.9.even_ref, f32[8,128]{1,0:T(8,128)S(1)} %collective-permute-done.10.odd_ref), custom_call_target="tpu_custom_call" | custom-call | tf_op jit(solution)/shard_map/pallas_call | solution.py:160
Async XLA Ops:
  0.6 1.0 %copy-start = (f32[1,256,512]{2,1,0:T(8,128)S(1)}, f32[1,256,512]{2,1,0:T(8,128)}, u32[]{:S(2)}) copy-start(f32[1,256,512]{2,1,0:T(8,128)} %param.4) | copy-start | bytes 1572868
  1.7 13.8 %copy-start.1 = (bf16[144,384]{1,0:T(8,128)(2,1)S(1)}, bf16[144,384]{1,0:T(8,128)(2,1)}, u32[]{:S(2)}) copy-start(bf16[144,384]{1,0:T(8,128)(2,1)} %constant.6.clone.left_ref) | copy-start | bytes 331780
  1.9 17.8 %collective-permute-start.3 = (f32[576,128]{1,0:T(8,128)S(1)}, f32[576,128]{1,0:T(8,128)S(1)}, u32[]{:S(2)}, u32[]{:S(2)}) collective-permute-start(f32[576,128]{1,0:T(8,128)S(1)} %get-tuple-element.11), channel_id=1, source_target_pairs={{0,16},{16,0},{17,1},{1,17},{2,18},{18,2},{19,3},{3,19},{4,20},{20... | collective-permute-start | bytes 884744 | tf_op jit(solution)/shard_map/ppermute | solution.py:250
  4.9 1.6 %collective-permute-start = (f32[32,512]{1,0:T(8,128)S(1)}, f32[32,512]{1,0:T(8,128)S(1)}, u32[]{:S(2)}, u32[]{:S(2)}) collective-permute-start(f32[32,512]{1,0:T(8,128)S(1)} %get-tuple-element.8), channel_id=1, source_target_pairs={{0,4},{4,0},{8,12},{12,8},{1,5},{5,1},{9,13},{13,9},{2,6},{6,2},{1... | collective-permute-start | bytes 196616 | tf_op jit(solution)/shard_map/ppermute | solution.py:271
  4.9 14.8 %copy-start.2 = (bf16[2,256,256]{2,1,0:T(8,128)(2,1)S(1)}, bf16[2,256,256]{2,1,0:T(8,128)(2,1)}, u32[]{:S(2)}) copy-start(bf16[2,256,256]{2,1,0:T(8,128)(2,1)} %constant.7.clone.right_ref) | copy-start | bytes 786436
  4.9 14.8 %copy-start.3 = (bf16[128,432]{1,0:T(8,128)(2,1)S(1)}, bf16[128,432]{1,0:T(8,128)(2,1)}, u32[]{:S(2)}) copy-start(bf16[128,432]{1,0:T(8,128)(2,1)} %constant.8.clone.back_ref) | copy-start | bytes 331780
  4.9 3.7 %collective-permute-start.1 = (f32[32,512]{1,0:T(8,128)S(1)}, f32[32,512]{1,0:T(8,128)S(1)}, u32[]{:S(2)}, u32[]{:S(2)}) collective-permute-start(f32[32,512]{1,0:T(8,128)S(1)} %get-tuple-element.9), channel_id=1, source_target_pairs={{0,12},{4,8},{8,4},{12,0},{1,13},{5,9},{9,5},{13,1},{2,14},{6,10},... | collective-permute-start | bytes 196616 | tf_op jit(solution)/shard_map/ppermute | solution.py:276
  8.8 10.8 %collective-permute-start.4 = (f32[144,128]{1,0:T(8,128)S(1)}, f32[144,128]{1,0:T(8,128)S(1)}, u32[]{:S(2)}, u32[]{:S(2)}) collective-permute-start(f32[144,128]{1,0:T(8,128)S(1)} %get-tuple-element.12), channel_id=1, source_target_pairs={{0,16},{16,0},{17,1},{1,17},{2,18},{18,2},{19,3},{3,19},{4,20},{20... | collective-permute-start | bytes 221192 | tf_op jit(solution)/shard_map/ppermute | solution.py:250
  9.7 5.8 %collective-permute-start.2 = (f32[80,128]{1,0:T(8,128)S(1)}, f32[80,128]{1,0:T(8,128)S(1)}, u32[]{:S(2)}, u32[]{:S(2)}) collective-permute-start(f32[80,128]{1,0:T(8,128)S(1)} %get-tuple-element.10), channel_id=1, source_target_pairs={{0,3},{16,17},{17,16},{1,2},{2,1},{18,19},{19,18},{3,0},{4,7},{20,... | collective-permute-start | bytes 122888 | tf_op jit(solution)/shard_map/ppermute | solution.py:250
  13.0 6.7 %collective-permute-start.5 = (f32[80,128]{1,0:T(8,128)S(1)}, f32[80,128]{1,0:T(8,128)S(1)}, u32[]{:S(2)}, u32[]{:S(2)}) collective-permute-start(f32[80,128]{1,0:T(8,128)S(1)} %get-tuple-element.13), channel_id=1, source_target_pairs={{0,17},{16,3},{17,2},{1,16},{2,19},{18,1},{19,0},{3,18},{4,21},{20... | collective-permute-start | bytes 122888 | tf_op jit(solution)/shard_map/ppermute | solution.py:250
  24.8 4.5 %collective-permute-start.8 = (f32[8,128]{1,0:T(8,128)S(1)}, f32[8,128]{1,0:T(8,128)S(1)}, u32[]{:S(2)}, u32[]{:S(2)}) collective-permute-start(f32[8,128]{1,0:T(8,128)S(1)} %shard_map.62.own_ref), channel_id=1, source_target_pairs={{0,19},{16,1},{17,0},{1,18},{2,17},{18,3},{19,2},{3,16},{4,23},{20... | collective-permute-start | bytes 12296 | tf_op jit(solution)/shard_map/ppermute | solution.py:250
  25.2 5.4 %collective-permute-start.7 = (f32[8,128]{1,0:T(8,128)S(1)}, f32[8,128]{1,0:T(8,128)S(1)}, u32[]{:S(2)}, u32[]{:S(2)}) collective-permute-start(f32[8,128]{1,0:T(8,128)S(1)} %shard_map.62.own_ref), channel_id=1, source_target_pairs={{0,3},{16,17},{17,16},{1,2},{2,1},{18,19},{19,18},{3,0},{4,7},{20,... | collective-permute-start | bytes 12296 | tf_op jit(solution)/shard_map/ppermute | solution.py:250
  26.0 4.7 %collective-permute-start.6 = (f32[8,128]{1,0:T(8,128)S(1)}, f32[8,128]{1,0:T(8,128)S(1)}, u32[]{:S(2)}, u32[]{:S(2)}) collective-permute-start(f32[8,128]{1,0:T(8,128)S(1)} %shard_map.62.own_ref), channel_id=1, source_target_pairs={{0,16},{16,0},{17,1},{1,17},{2,18},{18,2},{19,3},{3,19},{4,20},{20... | collective-permute-start | bytes 12296 | tf_op jit(solution)/shard_map/ppermute | solution.py:250
  30.7 3.0 %collective-permute-start.10 = (f32[8,128]{1,0:T(8,128)S(1)}, f32[8,128]{1,0:T(8,128)S(1)}, u32[]{:S(2)}, u32[]{:S(2)}) collective-permute-start(f32[8,128]{1,0:T(8,128)S(1)} %shard_map.63.own_ref), channel_id=1, source_target_pairs={{0,12},{4,8},{8,4},{12,0},{1,13},{5,9},{9,5},{13,1},{2,14},{6,10},... | collective-permute-start | bytes 12296 | tf_op jit(solution)/shard_map/ppermute | solution.py:276
  30.7 3.0 %collective-permute-start.9 = (f32[8,128]{1,0:T(8,128)S(1)}, f32[8,128]{1,0:T(8,128)S(1)}, u32[]{:S(2)}, u32[]{:S(2)}) collective-permute-start(f32[8,128]{1,0:T(8,128)S(1)} %shard_map.63.own_ref), channel_id=1, source_target_pairs={{0,4},{4,0},{8,12},{12,8},{1,5},{5,1},{9,13},{13,9},{2,6},{6,2},{1... | collective-permute-start | bytes 12296 | tf_op jit(solution)/shard_map/ppermute | solution.py:271

commit v3 on v2

--- a/solution.py
+++ b/solution.py
@@ -154,13 +154,14 @@
 IN_VMEM = pl.BlockSpec(memory_space=pltpu.VMEM)
 
 
-def kernel_call(body, outs, *args, scratch=(), last=False):
-    args = [pltpu.with_memory_space_constraint(a, pltpu.VMEM) if isinstance(a, jax.Array) else a for a in args]
+def kernel_call(body, outs, *args, scratch=(), first=False, last=False):
+    place = pltpu.HBM if first else pltpu.VMEM
+    args = [pltpu.with_memory_space_constraint(a, place) if isinstance(a, jax.Array) else a for a in args]
     shapes = outs if last else jax.tree.map(lambda out: pltpu.VMEM(out.shape, out.dtype), outs)
     return pl.pallas_call(
         body,
         out_shape=shapes,
-        in_specs=[IN_VMEM] * len(args),
+        in_specs=[pl.BlockSpec(memory_space=place)] * len(args),
         out_specs=jax.tree.map(lambda _: IN_VMEM, outs),
         scratch_shapes=scratch,
         compiler_params=pltpu.CompilerParams(vmem_limit_bytes=24 << 20),
@@ -171,7 +172,7 @@
     return jax.ShapeDtypeStruct(shape, jnp.float32)
 
 
-def flow_of(region, rows, cols, group=4):
+def flow_of(region, rows, cols, group=16):
     return kernel_call(
         functools.partial(flow_kernel, rows, cols, group),
         floats(2 * rows, PATCH), region, *tables(),
@@ -318,9 +319,17 @@
         pl.when(half == h)(functools.partial(branch, h))
 
 
-def cut_kernel(core, tile_ref, other_ref, even_ref, odd_ref):
+def cut_kernel(core, image_ref, tile_ref, other_ref, even_ref, odd_ref, sems):
     _, y, _, half = where_am_i()
     tall, width = tile_ref.shape
+    copies = []
+    for k in range(tall // HALF):
+        rows = pl.ds(k * HALF, HALF)
+        copies.append(pltpu.make_async_copy(image_ref.at[rows], tile_ref.at[rows], sems.at[k]))
+    for copy in copies:
+        copy.start()
+    for copy in copies:
+        copy.wait()
     lower = y % 2 == 1
     first, last = tile_ref[:HALF], tile_ref[tall - HALF:]
     even_ref[...] = jnp.where(lower, first, last)
@@ -444,8 +453,10 @@
     core, tall = half * STRIDE + HALF, tile.shape[0]
 
     strip = floats(HALF, tile.shape[1])
-    other, even, odd = kernel_call(
-        functools.partial(cut_kernel, core), (floats(tall * core // PATCH, PATCH), strip, strip), tile,
+    tile, other, even, odd = kernel_call(
+        functools.partial(cut_kernel, core),
+        (floats(*tile.shape), floats(tall * core // PATCH, PATCH), strip, strip), tile,
+        scratch=[pltpu.SemaphoreType.DMA((tall // HALF,))], first=True,
     )
     other = along(other, mate)
     even, odd = pairs_even(even), pairs_odd(odd)
@@ -463,7 +474,7 @@
         scratch=region_scratch(rows, half),
     )
     flow = kernel_call(
-        functools.partial(pair_kernel, rows, half, 4, nx), floats(2 * rows, PATCH),
+        functools.partial(pair_kernel, rows, half, rows * half, nx), floats(2 * rows, PATCH),
         own, other, strips, cross, left, right, back,
         scratch=region_scratch(rows, half) + [pltpu.VMEM(spectra, jnp.float32)] + stats_scratch(rows, half),
     )

time: 34.8 us -> 33.9 us (0.974)
  local copies, waits for them, and re-layouts: 1.05 us -> 0.01 us
    unnamed x8 -> x6, local copies, waits for them, and re-layouts: 1.05 us -> 0.01 us
  transfers between devices with their start and end apart: 11 -> 11, of which waited for: 6 -> 6; matrix products, arithmetic and copies ran while one was open for 0% -> 0% of each run, Pallas kernels for 3% -> 4%
where the time goes in v3:
time: 33.9 us; the launch traced here: 33.8 us
  starting transfers between devices  13.8 us (41%)
  waiting for transfers between devices  11.6 us (34%)
  Pallas kernels  7.62 us (22%)
  between operations  0.69 us (2%)
    ppermute x7, starting transfers between devices, along(): return lax.ppermute(value, AXES, pairs)  10.6 us
    ppermute x7, waiting for transfers between devices, along(): return lax.ppermute(value, AXES, pairs)  8.11 us
    pallas_call x6, Pallas kernels, kernel_call(): pl.pallas_call(body, out_shape=shapes, in_specs=[pl.BlockSpec(memory_spac...  7.62 us
    ppermute x2, waiting for transfers between devices, pairs_odd(): lax.ppermute(value, 'ty', [(i, (i - 1 if i % 2 == 0 else i + 1) % size) f...  3.52 us
    ppermute x2, starting transfers between devices, pairs_odd(): lax.ppermute(value, 'ty', [(i, (i - 1 if i % 2 == 0 else i + 1) % size) f...  1.62 us
    ppermute x2, starting transfers between devices, pairs_even(): return lax.ppermute(value, 'ty', [(i, i ^ 1) for i in range(size)])  1.6 us
  transfers between devices with their start and end apart: 11, of which 6 were waited for; matrix products, arithmetic and copies ran while one was open for 0% of the time, Pallas kernels for 4%

profile of v3, /device:TPU:0, one launch (start us, length us, event | category | flops | bytes accessed | tf_op | source)
XLA Modules:
  0.0 33.8 jit_solution(12533745410830823067)
XLA Ops:
  0.6 0.0 copy-start
  0.6 1.4 %shard_map.59 = (f32[256,512]{1,0:T(8,128)S(1)}, f32[576,128]{1,0:T(8,128)S(1)}, f32[32,512]{1,0:T(8,128)S(1)}, f32[32,512]{1,0:T(8,128)S(1)}) custom-call(f32[256,512]{1,0:T(8,128)} %bitcast.1), custom_call_target="tpu_custom_call" | custom-call | tf_op jit(solution)/shard_map/pallas_call | solution.py:161
  2.0 2.9 %collective-permute-start.3 = (f32[576,128]{1,0:T(8,128)S(1)}, f32[576,128]{1,0:T(8,128)S(1)}, u32[]{:S(2)}, u32[]{:S(2)}) collective-permute-start(f32[576,128]{1,0:T(8,128)S(1)} %get-tuple-element.13), channel_id=1, source_target_pairs={{0,16},{16,0},{17,1},{1,17},{2,18},{18,2},{19,3},{3,19},{4,20},{20... | collective-permute-start | bytes 884744 | tf_op jit(solution)/shard_map/ppermute | solution.py:251
  5.0 0.0 collective-permute-start
  5.0 1.6 %collective-permute-start.1 = (f32[32,512]{1,0:T(8,128)S(1)}, f32[32,512]{1,0:T(8,128)S(1)}, u32[]{:S(2)}, u32[]{:S(2)}) collective-permute-start(f32[32,512]{1,0:T(8,128)S(1)} %get-tuple-element.11), channel_id=1, source_target_pairs={{0,12},{4,8},{8,4},{12,0},{1,13},{5,9},{9,5},{13,1},{2,14},{6,10},... | collective-permute-start | bytes 196616 | tf_op jit(solution)/shard_map/ppermute | solution.py:277
  6.6 0.0 collective-permute-done.even_ref
  6.6 2.1 %collective-permute-done.1.odd_ref = f32[32,512]{1,0:T(8,128)S(1)} collective-permute-done((f32[32,512]{1,0:T(8,128)S(1)}, f32[32,512]{1,0:T(8,128)S(1)}, u32[]{:S(2)}, u32[]{:S(2)}) %collective-permute-start.1) | collective-permute-done | bytes 65568 | tf_op jit(solution)/shard_map/ppermute | solution.py:277
  8.7 0.0 copy-start.1
  8.7 0.0 copy-start.2
  8.7 0.3 shard_map.60
  9.0 0.9 %collective-permute-start.4 = (f32[144,128]{1,0:T(8,128)S(1)}, f32[144,128]{1,0:T(8,128)S(1)}, u32[]{:S(2)}, u32[]{:S(2)}) collective-permute-start(f32[144,128]{1,0:T(8,128)S(1)} %get-tuple-element.14), channel_id=1, source_target_pairs={{0,16},{16,0},{17,1},{1,17},{2,18},{18,2},{19,3},{3,19},{4,20},{20... | collective-permute-start | bytes 221192 | tf_op jit(solution)/shard_map/ppermute | solution.py:251
  9.8 3.3 %collective-permute-start.2 = (f32[80,128]{1,0:T(8,128)S(1)}, f32[80,128]{1,0:T(8,128)S(1)}, u32[]{:S(2)}, u32[]{:S(2)}) collective-permute-start(f32[80,128]{1,0:T(8,128)S(1)} %get-tuple-element.12), channel_id=1, source_target_pairs={{0,3},{16,17},{17,16},{1,2},{2,1},{18,19},{19,18},{3,0},{4,7},{20,... | collective-permute-start | bytes 122888 | tf_op jit(solution)/shard_map/ppermute | solution.py:251
  13.1 0.0 collective-permute-start.5
  13.1 2.5 %collective-permute-done.2.side_ref = f32[80,128]{1,0:T(8,128)S(1)} collective-permute-done((f32[80,128]{1,0:T(8,128)S(1)}, f32[80,128]{1,0:T(8,128)S(1)}, u32[]{:S(2)}, u32[]{:S(2)}) %collective-permute-start.2) | collective-permute-done | bytes 40992 | tf_op jit(solution)/shard_map/ppermute | solution.py:251
  15.6 0.0 copy-done
  15.6 0.9 %shard_map.61.own_ref = f32[16,72,256]{2,1,0:T(8,128)S(1)} custom-call(f32[256,512]{1,0:T(8,128)S(1)} %get-tuple-element.9.tile_ref, f32[32,512]{1,0:T(8,128)S(1)} %collective-permute-done.even_ref, f32[32,512]{1,0:T(8,128)S(1)} %collective-permute-done.1.odd_ref, f32[80,128]{1,0:T(8,128)S(1)} %collective-permute-done.2.side_ref, bf16[144,384]{1,0:T(8,128)(2,1)S(1)} %copy-done), custom_call_target="tpu_custom_call" | custom-call | tf_op jit(solution)/shard_map/pallas_call | solution.py:161
  16.6 3.2 %collective-permute-done.5.cross_ref = f32[80,128]{1,0:T(8,128)S(1)} collective-permute-done((f32[80,128]{1,0:T(8,128)S(1)}, f32[80,128]{1,0:T(8,128)S(1)}, u32[]{:S(2)}, u32[]{:S(2)}) %collective-permute-start.5) | collective-permute-done | bytes 40992 | tf_op jit(solution)/shard_map/ppermute | solution.py:251
  19.8 0.0 collective-permute-done.4.strips_ref
  19.8 0.0 collective-permute-done.3.other_ref
  19.8 0.0 copy-done.1
  19.8 0.0 copy-done.2
  19.8 4.1 %shard_map.62.own_ref = f32[8,128]{1,0:T(8,128)S(1)} custom-call(f32[16,72,256]{2,1,0:T(8,128)S(1)} %shard_map.61.own_ref, f32[576,128]{1,0:T(8,128)S(1)} %collective-permute-done.3.other_ref, f32[144,128]{1,0:T(8,128)S(1)} %collective-permute-done.4.strips_ref, f32[80,128]{1,0:T(8,128)S(1)} %collective-permute-done.5.cross_ref, ...), custom_call_target="tpu_custom_call" | custom-call | tf_op jit(solution)/shard_map/pallas_call | solution.py:161
  23.9 0.5 %collective-permute-start.8 = (f32[8,128]{1,0:T(8,128)S(1)}, f32[8,128]{1,0:T(8,128)S(1)}, u32[]{:S(2)}, u32[]{:S(2)}) collective-permute-start(f32[8,128]{1,0:T(8,128)S(1)} %shard_map.62.own_ref), channel_id=1, source_target_pairs={{0,19},{16,1},{17,0},{1,18},{2,17},{18,3},{19,2},{3,16},{4,23},{20... | collective-permute-start | bytes 12296 | tf_op jit(solution)/shard_map/ppermute | solution.py:251
  24.4 0.7 %collective-permute-start.7 = (f32[8,128]{1,0:T(8,128)S(1)}, f32[8,128]{1,0:T(8,128)S(1)}, u32[]{:S(2)}, u32[]{:S(2)}) collective-permute-start(f32[8,128]{1,0:T(8,128)S(1)} %shard_map.62.own_ref), channel_id=1, source_target_pairs={{0,3},{16,17},{17,16},{1,2},{2,1},{18,19},{19,18},{3,0},{4,7},{20,... | collective-permute-start | bytes 12296 | tf_op jit(solution)/shard_map/ppermute | solution.py:251
  25.1 2.3 %collective-permute-start.6 = (f32[8,128]{1,0:T(8,128)S(1)}, f32[8,128]{1,0:T(8,128)S(1)}, u32[]{:S(2)}, u32[]{:S(2)}) collective-permute-start(f32[8,128]{1,0:T(8,128)S(1)} %shard_map.62.own_ref), channel_id=1, source_target_pairs={{0,16},{16,0},{17,1},{1,17},{2,18},{18,2},{19,3},{3,19},{4,20},{20... | collective-permute-start | bytes 12296 | tf_op jit(solution)/shard_map/ppermute | solution.py:251
  27.5 1.0 %collective-permute-done.8.far_ref = f32[8,128]{1,0:T(8,128)S(1)} collective-permute-done((f32[8,128]{1,0:T(8,128)S(1)}, f32[8,128]{1,0:T(8,128)S(1)}, u32[]{:S(2)}, u32[]{:S(2)}) %collective-permute-start.8) | collective-permute-done | bytes 4128 | tf_op jit(solution)/shard_map/ppermute | solution.py:251
  28.5 1.3 %collective-permute-done.7.near_ref = f32[8,128]{1,0:T(8,128)S(1)} collective-permute-done((f32[8,128]{1,0:T(8,128)S(1)}, f32[8,128]{1,0:T(8,128)S(1)}, u32[]{:S(2)}, u32[]{:S(2)}) %collective-permute-start.7) | collective-permute-done | bytes 4128 | tf_op jit(solution)/shard_map/ppermute | solution.py:251
  29.8 0.0 collective-permute-done.6.mate_ref
  29.8 0.1 shard_map.63.own_ref
  29.9 0.0 collective-permute-start.10
  29.9 1.6 %collective-permute-start.9 = (f32[8,128]{1,0:T(8,128)S(1)}, f32[8,128]{1,0:T(8,128)S(1)}, u32[]{:S(2)}, u32[]{:S(2)}) collective-permute-start(f32[8,128]{1,0:T(8,128)S(1)} %shard_map.63.own_ref), channel_id=1, source_target_pairs={{0,4},{4,0},{8,12},{12,8},{1,5},{5,1},{9,13},{13,9},{2,6},{6,2},{1... | collective-permute-start | bytes 12296 | tf_op jit(solution)/shard_map/ppermute | solution.py:272
  31.5 1.4 %collective-permute-done.10.odd_ref = f32[8,128]{1,0:T(8,128)S(1)} collective-permute-done((f32[8,128]{1,0:T(8,128)S(1)}, f32[8,128]{1,0:T(8,128)S(1)}, u32[]{:S(2)}, u32[]{:S(2)}) %collective-permute-start.10) | collective-permute-done | bytes 4128 | tf_op jit(solution)/shard_map/ppermute | solution.py:277
  32.9 0.0 collective-permute-done.9.even_ref
  32.9 0.8 %shard_map.64 = (f32[1,2,4,8]{3,2,1,0:T(4,128)}, f32[1,2,4,8]{3,2,1,0:T(4,128)}) custom-call(f32[8,128]{1,0:T(8,128)S(1)} %shard_map.63.own_ref, f32[8,128]{1,0:T(8,128)S(1)} %collective-permute-done.9.even_ref, f32[8,128]{1,0:T(8,128)S(1)} %collective-permute-done.10.odd_ref), custom_call_target="tpu_custom_call" | custom-call | tf_op jit(solution)/shard_map/pallas_call | solution.py:161
Async XLA Ops:
  0.6 15.0 %copy-start = (bf16[144,384]{1,0:T(8,128)(2,1)S(1)}, bf16[144,384]{1,0:T(8,128)(2,1)}, u32[]{:S(2)}) copy-start(bf16[144,384]{1,0:T(8,128)(2,1)} %constant.6.clone.left_ref) | copy-start | bytes 331780
  2.0 17.8 %collective-permute-start.3 = (f32[576,128]{1,0:T(8,128)S(1)}, f32[576,128]{1,0:T(8,128)S(1)}, u32[]{:S(2)}, u32[]{:S(2)}) collective-permute-start(f32[576,128]{1,0:T(8,128)S(1)} %get-tuple-element.13), channel_id=1, source_target_pairs={{0,16},{16,0},{17,1},{1,17},{2,18},{18,2},{19,3},{3,19},{4,20},{20... | collective-permute-start | bytes 884744 | tf_op jit(solution)/shard_map/ppermute | solution.py:251
  5.0 1.6 %collective-permute-start = (f32[32,512]{1,0:T(8,128)S(1)}, f32[32,512]{1,0:T(8,128)S(1)}, u32[]{:S(2)}, u32[]{:S(2)}) collective-permute-start(f32[32,512]{1,0:T(8,128)S(1)} %get-tuple-element.10), channel_id=1, source_target_pairs={{0,4},{4,0},{8,12},{12,8},{1,5},{5,1},{9,13},{13,9},{2,6},{6,2},{1... | collective-permute-start | bytes 196616 | tf_op jit(solution)/shard_map/ppermute | solution.py:272
  5.0 3.7 %collective-permute-start.1 = (f32[32,512]{1,0:T(8,128)S(1)}, f32[32,512]{1,0:T(8,128)S(1)}, u32[]{:S(2)}, u32[]{:S(2)}) collective-permute-start(f32[32,512]{1,0:T(8,128)S(1)} %get-tuple-element.11), channel_id=1, source_target_pairs={{0,12},{4,8},{8,4},{12,0},{1,13},{5,9},{9,5},{13,1},{2,14},{6,10},... | collective-permute-start | bytes 196616 | tf_op jit(solution)/shard_map/ppermute | solution.py:277
  8.7 11.1 %copy-start.1 = (bf16[2,256,256]{2,1,0:T(8,128)(2,1)S(1)}, bf16[2,256,256]{2,1,0:T(8,128)(2,1)}, u32[]{:S(2)}) copy-start(bf16[2,256,256]{2,1,0:T(8,128)(2,1)} %constant.7.clone.right_ref) | copy-start | bytes 786436
  8.7 11.1 %copy-start.2 = (bf16[128,432]{1,0:T(8,128)(2,1)S(1)}, bf16[128,432]{1,0:T(8,128)(2,1)}, u32[]{:S(2)}) copy-start(bf16[128,432]{1,0:T(8,128)(2,1)} %constant.8.clone.back_ref) | copy-start | bytes 331780
  9.0 10.8 %collective-permute-start.4 = (f32[144,128]{1,0:T(8,128)S(1)}, f32[144,128]{1,0:T(8,128)S(1)}, u32[]{:S(2)}, u32[]{:S(2)}) collective-permute-start(f32[144,128]{1,0:T(8,128)S(1)} %get-tuple-element.14), channel_id=1, source_target_pairs={{0,16},{16,0},{17,1},{1,17},{2,18},{18,2},{19,3},{3,19},{4,20},{20... | collective-permute-start | bytes 221192 | tf_op jit(solution)/shard_map/ppermute | solution.py:251
  9.8 5.8 %collective-permute-start.2 = (f32[80,128]{1,0:T(8,128)S(1)}, f32[80,128]{1,0:T(8,128)S(1)}, u32[]{:S(2)}, u32[]{:S(2)}) collective-permute-start(f32[80,128]{1,0:T(8,128)S(1)} %get-tuple-element.12), channel_id=1, source_target_pairs={{0,3},{16,17},{17,16},{1,2},{2,1},{18,19},{19,18},{3,0},{4,7},{20,... | collective-permute-start | bytes 122888 | tf_op jit(solution)/shard_map/ppermute | solution.py:251
  13.1 6.7 %collective-permute-start.5 = (f32[80,128]{1,0:T(8,128)S(1)}, f32[80,128]{1,0:T(8,128)S(1)}, u32[]{:S(2)}, u32[]{:S(2)}) collective-permute-start(f32[80,128]{1,0:T(8,128)S(1)} %get-tuple-element.15), channel_id=1, source_target_pairs={{0,17},{16,3},{17,2},{1,16},{2,19},{18,1},{19,0},{3,18},{4,21},{20... | collective-permute-start | bytes 122888 | tf_op jit(solution)/shard_map/ppermute | solution.py:251
  23.9 4.5 %collective-permute-start.8 = (f32[8,128]{1,0:T(8,128)S(1)}, f32[8,128]{1,0:T(8,128)S(1)}, u32[]{:S(2)}, u32[]{:S(2)}) collective-permute-start(f32[8,128]{1,0:T(8,128)S(1)} %shard_map.62.own_ref), channel_id=1, source_target_pairs={{0,19},{16,1},{17,0},{1,18},{2,17},{18,3},{19,2},{3,16},{4,23},{20... | collective-permute-start | bytes 12296 | tf_op jit(solution)/shard_map/ppermute | solution.py:251
  24.4 5.4 %collective-permute-start.7 = (f32[8,128]{1,0:T(8,128)S(1)}, f32[8,128]{1,0:T(8,128)S(1)}, u32[]{:S(2)}, u32[]{:S(2)}) collective-permute-start(f32[8,128]{1,0:T(8,128)S(1)} %shard_map.62.own_ref), channel_id=1, source_target_pairs={{0,3},{16,17},{17,16},{1,2},{2,1},{18,19},{19,18},{3,0},{4,7},{20,... | collective-permute-start | bytes 12296 | tf_op jit(solution)/shard_map/ppermute | solution.py:251
  25.1 4.7 %collective-permute-start.6 = (f32[8,128]{1,0:T(8,128)S(1)}, f32[8,128]{1,0:T(8,128)S(1)}, u32[]{:S(2)}, u32[]{:S(2)}) collective-permute-start(f32[8,128]{1,0:T(8,128)S(1)} %shard_map.62.own_ref), channel_id=1, source_target_pairs={{0,16},{16,0},{17,1},{1,17},{2,18},{18,2},{19,3},{3,19},{4,20},{20... | collective-permute-start | bytes 12296 | tf_op jit(solution)/shard_map/ppermute | solution.py:251
  29.9 3.0 %collective-permute-start.10 = (f32[8,128]{1,0:T(8,128)S(1)}, f32[8,128]{1,0:T(8,128)S(1)}, u32[]{:S(2)}, u32[]{:S(2)}) collective-permute-start(f32[8,128]{1,0:T(8,128)S(1)} %shard_map.63.own_ref), channel_id=1, source_target_pairs={{0,12},{4,8},{8,4},{12,0},{1,13},{5,9},{9,5},{13,1},{2,14},{6,10},... | collective-permute-start | bytes 12296 | tf_op jit(solution)/shard_map/ppermute | solution.py:277
  29.9 3.0 %collective-permute-start.9 = (f32[8,128]{1,0:T(8,128)S(1)}, f32[8,128]{1,0:T(8,128)S(1)}, u32[]{:S(2)}, u32[]{:S(2)}) collective-permute-start(f32[8,128]{1,0:T(8,128)S(1)} %shard_map.63.own_ref), channel_id=1, source_target_pairs={{0,4},{4,0},{8,12},{12,8},{1,5},{5,1},{9,13},{13,9},{2,6},{6,2},{1... | collective-permute-start | bytes 12296 | tf_op jit(solution)/shard_map/ppermute | solution.py:272

commit v4 on v2

--- a/solution.py
+++ b/solution.py
@@ -171,7 +171,7 @@
     return jax.ShapeDtypeStruct(shape, jnp.float32)
 
 
-def flow_of(region, rows, cols, group=4):
+def flow_of(region, rows, cols, group=16):
     return kernel_call(
         functools.partial(flow_kernel, rows, cols, group),
         floats(2 * rows, PATCH), region, *tables(),
@@ -245,25 +245,28 @@
     pairs = []
     for y in range(ny):
         for g in range(2 * nx):
-            to = step(g) % (2 * nx)
+            to = step(g, 2 * nx)
             pairs.append((placed(g % 2, y, g // 2), placed(to % 2, y, to // 2)))
     return lax.ppermute(value, AXES, pairs)
 
 
-def mate(g):
+def mate(g, count):
     return g ^ 1
 
 
-def near(g):
-    return g - 1 if g % 2 == 0 else g + 1
-
-
-def far(g):
-    return g - 2 if g % 2 == 0 else g + 2
-
-
-def past(g):
-    return g + 2 if g % 2 == 0 else g - 2
+def near(g, count):
+    to = g - 1 if g % 2 == 0 else g + 1
+    return to if 0 <= to < count else g
+
+
+def far(g, count):
+    to = g - 2 if g % 2 == 0 else g + 2
+    return to if 0 <= to < count else g ^ 1
+
+
+def past(g, count):
+    to = g + 2 if g % 2 == 0 else g - 2
+    return to if 0 <= to < count else g ^ 1
 
 
 def pairs_even(value):
@@ -273,7 +276,8 @@
 
 def pairs_odd(value):
     size = lax.axis_size("ty")
-    return lax.ppermute(value, "ty", [(i, (i - 1 if i % 2 == 0 else i + 1) % size) for i in range(size)])
+    to = [i - 1 if i % 2 == 0 else i + 1 for i in range(size)]
+    return lax.ppermute(value, "ty", [(i, t if 0 <= t < size else i) for i, t in enumerate(to)])
 
 
 def around(y, ny, even, odd):
@@ -463,7 +467,7 @@
         scratch=region_scratch(rows, half),
     )
     flow = kernel_call(
-        functools.partial(pair_kernel, rows, half, 4, nx), floats(2 * rows, PATCH),
+        functools.partial(pair_kernel, rows, half, rows * half, nx), floats(2 * rows, PATCH),
         own, other, strips, cross, left, right, back,
         scratch=region_scratch(rows, half) + [pltpu.VMEM(spectra, jnp.float32)] + stats_scratch(rows, half),
     )

time: 34.8 us -> 37.2 us (1.069)
  the two profiles are of different devices: /device:TPU:0 before, /device:TPU:17 now
where the time goes in v4:
time: 37.2 us; the launch traced here: 36.9 us
  starting transfers between devices  21.6 us (58%)
  waiting for transfers between devices  7.07 us (19%)
  Pallas kernels  6.45 us (17%)
  local copies, waits for them, and re-layouts  1.05 us (3%)
  between operations  0.74 us (2%)
    ppermute x7, starting transfers between devices, along(): return lax.ppermute(value, AXES, pairs)  11.4 us
    ppermute x2, starting transfers between devices, pairs_odd(): lax.ppermute(value, 'ty', [(i, t if 0 <= t < size else i) for i, t in enu...  9.26 us
    pallas_call x6, Pallas kernels, kernel_call(): pl.pallas_call(body, out_shape=shapes, in_specs=[IN_VMEM] * len(args), ou...  6.45 us
    ppermute x2, waiting for transfers between devices, pairs_odd(): lax.ppermute(value, 'ty', [(i, t if 0 <= t < size else i) for i, t in enu...  4.05 us
    ppermute x7, waiting for transfers between devices, along(): return lax.ppermute(value, AXES, pairs)  3.01 us
    unnamed x8, local copies, waits for them, and re-layouts  1.05 us
    ppermute x2, starting transfers between devices, pairs_even(): return lax.ppermute(value, 'ty', [(i, i ^ 1) for i in range(size)])  1.03 us
  transfers between devices with their start and end apart: 11, of which 6 were waited for; matrix products, arithmetic and copies ran while one was open for 0% of the time, Pallas kernels for 3%

profile of v4, /device:TPU:17, one launch (start us, length us, event | category | flops | bytes accessed | tf_op | source)
XLA Modules:
  0.0 36.9 jit_solution(2711899330513730154)
XLA Ops:
  0.6 0.0 copy-start
  0.6 1.0 %copy-done = f32[1,256,512]{2,1,0:T(8,128)S(1)} copy-done((f32[1,256,512]{2,1,0:T(8,128)S(1)}, f32[1,256,512]{2,1,0:T(8,128)}, u32[]{:S(2)}) %copy-start) | copy-done | bytes 524312
  1.7 0.0 copy-start.1
  1.7 0.2 shard_map.59
  1.9 1.2 %collective-permute-start.3 = (f32[576,128]{1,0:T(8,128)S(1)}, f32[576,128]{1,0:T(8,128)S(1)}, u32[]{:S(2)}, u32[]{:S(2)}) collective-permute-start(f32[576,128]{1,0:T(8,128)S(1)} %get-tuple-element.11), channel_id=1, source_target_pairs={{0,16},{16,0},{17,1},{1,17},{2,18},{18,2},{19,3},{3,19},{4,20},{20... | collective-permute-start | bytes 884744 | tf_op jit(solution)/shard_map/ppermute | solution.py:250
  3.1 1.0 %collective-permute-start = (f32[32,512]{1,0:T(8,128)S(1)}, f32[32,512]{1,0:T(8,128)S(1)}, u32[]{:S(2)}, u32[]{:S(2)}) collective-permute-start(f32[32,512]{1,0:T(8,128)S(1)} %get-tuple-element.8), channel_id=1, source_target_pairs={{0,4},{4,0},{8,12},{12,8},{1,5},{5,1},{9,13},{13,9},{2,6},{6,2},{1... | collective-permute-start | bytes 196616 | tf_op jit(solution)/shard_map/ppermute | solution.py:274
  4.1 0.0 copy-start.2
  4.1 0.0 copy-start.3
  4.1 3.1 %collective-permute-start.1 = (f32[32,512]{1,0:T(8,128)S(1)}, f32[32,512]{1,0:T(8,128)S(1)}, u32[]{:S(2)}, u32[]{:S(2)}) collective-permute-start(f32[32,512]{1,0:T(8,128)S(1)} %get-tuple-element.9), channel_id=1, source_target_pairs={{0,0},{4,8},{8,4},{12,12},{1,1},{5,9},{9,5},{13,13},{2,2},{6,10},{... | collective-permute-start | bytes 196616 | tf_op jit(solution)/shard_map/ppermute | solution.py:280
  7.2 0.0 collective-permute-done.even_ref
  7.2 2.9 %collective-permute-done.1.odd_ref = f32[32,512]{1,0:T(8,128)S(1)} collective-permute-done((f32[32,512]{1,0:T(8,128)S(1)}, f32[32,512]{1,0:T(8,128)S(1)}, u32[]{:S(2)}, u32[]{:S(2)}) %collective-permute-start.1) | collective-permute-done | bytes 65568 | tf_op jit(solution)/shard_map/ppermute | solution.py:280
  10.1 0.3 shard_map.60
  10.3 0.3 collective-permute-start.4
  10.6 2.0 %collective-permute-start.2 = (f32[80,128]{1,0:T(8,128)S(1)}, f32[80,128]{1,0:T(8,128)S(1)}, u32[]{:S(2)}, u32[]{:S(2)}) collective-permute-start(f32[80,128]{1,0:T(8,128)S(1)} %get-tuple-element.10), channel_id=1, source_target_pairs={{0,0},{16,17},{17,16},{1,2},{2,1},{18,19},{19,18},{3,3},{4,4},{20,... | collective-permute-start | bytes 122888 | tf_op jit(solution)/shard_map/ppermute | solution.py:250
  12.7 2.3 %collective-permute-start.5 = (f32[80,128]{1,0:T(8,128)S(1)}, f32[80,128]{1,0:T(8,128)S(1)}, u32[]{:S(2)}, u32[]{:S(2)}) collective-permute-start(f32[80,128]{1,0:T(8,128)S(1)} %get-tuple-element.13), channel_id=1, source_target_pairs={{0,17},{16,0},{17,2},{1,16},{2,19},{18,1},{19,3},{3,18},{4,21},{20... | collective-permute-start | bytes 122888 | tf_op jit(solution)/shard_map/ppermute | solution.py:250
  15.0 0.4 %collective-permute-done.2.side_ref = f32[80,128]{1,0:T(8,128)S(1)} collective-permute-done((f32[80,128]{1,0:T(8,128)S(1)}, f32[80,128]{1,0:T(8,128)S(1)}, u32[]{:S(2)}, u32[]{:S(2)}) %collective-permute-start.2) | collective-permute-done | bytes 40992 | tf_op jit(solution)/shard_map/ppermute | solution.py:250
  15.4 0.0 copy-done.1
  15.4 0.9 %shard_map.61.own_ref = f32[16,72,256]{2,1,0:T(8,128)S(1)} custom-call(f32[256,512]{1,0:T(8,128)S(1)} %bitcast.3, f32[32,512]{1,0:T(8,128)S(1)} %collective-permute-done.even_ref, f32[32,512]{1,0:T(8,128)S(1)} %collective-permute-done.1.odd_ref, f32[80,128]{1,0:T(8,128)S(1)} %collective-permute-done.2.side_ref, bf16[144,384]{1,0:T(8,128)(2,1)S(1)} %copy-done.1), custom_call_target="tpu_custom_call" | custom-call | tf_op jit(solution)/shard_map/pallas_call | solution.py:160
  16.3 0.2 collective-permute-done.5.cross_ref
  16.5 0.0 collective-permute-done.4.strips_ref
  16.5 0.0 collective-permute-done.3.other_ref
  16.5 0.0 copy-done.2
  16.5 0.0 copy-done.3
  16.5 4.1 %shard_map.62.own_ref = f32[8,128]{1,0:T(8,128)S(1)} custom-call(f32[16,72,256]{2,1,0:T(8,128)S(1)} %shard_map.61.own_ref, f32[576,128]{1,0:T(8,128)S(1)} %collective-permute-done.3.other_ref, f32[144,128]{1,0:T(8,128)S(1)} %collective-permute-done.4.strips_ref, f32[80,128]{1,0:T(8,128)S(1)} %collective-permute-done.5.cross_ref, ...), custom_call_target="tpu_custom_call" | custom-call | tf_op jit(solution)/shard_map/pallas_call | solution.py:160
  20.6 1.2 %collective-permute-start.8 = (f32[8,128]{1,0:T(8,128)S(1)}, f32[8,128]{1,0:T(8,128)S(1)}, u32[]{:S(2)}, u32[]{:S(2)}) collective-permute-start(f32[8,128]{1,0:T(8,128)S(1)} %shard_map.62.own_ref), channel_id=1, source_target_pairs={{0,16},{16,1},{17,0},{1,18},{2,17},{18,3},{19,2},{3,19},{4,20},{20... | collective-permute-start | bytes 12296 | tf_op jit(solution)/shard_map/ppermute | solution.py:250
  21.8 4.3 %collective-permute-start.7 = (f32[8,128]{1,0:T(8,128)S(1)}, f32[8,128]{1,0:T(8,128)S(1)}, u32[]{:S(2)}, u32[]{:S(2)}) collective-permute-start(f32[8,128]{1,0:T(8,128)S(1)} %shard_map.62.own_ref), channel_id=1, source_target_pairs={{0,0},{16,17},{17,16},{1,2},{2,1},{18,19},{19,18},{3,3},{4,4},{20,... | collective-permute-start | bytes 12296 | tf_op jit(solution)/shard_map/ppermute | solution.py:250
  26.1 0.1 collective-permute-start.6
  26.2 0.0 collective-permute-done.8.far_ref
  26.2 0.9 %collective-permute-done.7.near_ref = f32[8,128]{1,0:T(8,128)S(1)} collective-permute-done((f32[8,128]{1,0:T(8,128)S(1)}, f32[8,128]{1,0:T(8,128)S(1)}, u32[]{:S(2)}, u32[]{:S(2)}) %collective-permute-start.7) | collective-permute-done | bytes 4128 | tf_op jit(solution)/shard_map/ppermute | solution.py:250
  27.1 1.5 %collective-permute-done.6.mate_ref = f32[8,128]{1,0:T(8,128)S(1)} collective-permute-done((f32[8,128]{1,0:T(8,128)S(1)}, f32[8,128]{1,0:T(8,128)S(1)}, u32[]{:S(2)}, u32[]{:S(2)}) %collective-permute-start.6) | collective-permute-done | bytes 4128 | tf_op jit(solution)/shard_map/ppermute | solution.py:250
  28.6 0.1 shard_map.63.own_ref
  28.7 6.1 %collective-permute-start.10 = (f32[8,128]{1,0:T(8,128)S(1)}, f32[8,128]{1,0:T(8,128)S(1)}, u32[]{:S(2)}, u32[]{:S(2)}) collective-permute-start(f32[8,128]{1,0:T(8,128)S(1)} %shard_map.63.own_ref), channel_id=1, source_target_pairs={{0,0},{4,8},{8,4},{12,12},{1,1},{5,9},{9,5},{13,13},{2,2},{6,10},{... | collective-permute-start | bytes 12296 | tf_op jit(solution)/shard_map/ppermute | solution.py:280
  34.8 0.1 collective-permute-start.9
  34.9 1.2 %collective-permute-done.10.odd_ref = f32[8,128]{1,0:T(8,128)S(1)} collective-permute-done((f32[8,128]{1,0:T(8,128)S(1)}, f32[8,128]{1,0:T(8,128)S(1)}, u32[]{:S(2)}, u32[]{:S(2)}) %collective-permute-start.10) | collective-permute-done | bytes 4128 | tf_op jit(solution)/shard_map/ppermute | solution.py:280
  36.1 0.0 collective-permute-done.9.even_ref
  36.1 0.8 %shard_map.64 = (f32[1,2,4,8]{3,2,1,0:T(4,128)}, f32[1,2,4,8]{3,2,1,0:T(4,128)}) custom-call(f32[8,128]{1,0:T(8,128)S(1)} %shard_map.63.own_ref, f32[8,128]{1,0:T(8,128)S(1)} %collective-permute-done.9.even_ref, f32[8,128]{1,0:T(8,128)S(1)} %collective-permute-done.10.odd_ref), custom_call_target="tpu_custom_call" | custom-call | tf_op jit(solution)/shard_map/pallas_call | solution.py:160
Async XLA Ops:
  0.6 1.0 %copy-start = (f32[1,256,512]{2,1,0:T(8,128)S(1)}, f32[1,256,512]{2,1,0:T(8,128)}, u32[]{:S(2)}) copy-start(f32[1,256,512]{2,1,0:T(8,128)} %param.4) | copy-start | bytes 1572868
  1.7 13.7 %copy-start.1 = (bf16[144,384]{1,0:T(8,128)(2,1)S(1)}, bf16[144,384]{1,0:T(8,128)(2,1)}, u32[]{:S(2)}) copy-start(bf16[144,384]{1,0:T(8,128)(2,1)} %constant.6.clone.left_ref) | copy-start | bytes 331780
  1.9 14.6 %collective-permute-start.3 = (f32[576,128]{1,0:T(8,128)S(1)}, f32[576,128]{1,0:T(8,128)S(1)}, u32[]{:S(2)}, u32[]{:S(2)}) collective-permute-start(f32[576,128]{1,0:T(8,128)S(1)} %get-tuple-element.11), channel_id=1, source_target_pairs={{0,16},{16,0},{17,1},{1,17},{2,18},{18,2},{19,3},{3,19},{4,20},{20... | collective-permute-start | bytes 884744 | tf_op jit(solution)/shard_map/ppermute | solution.py:250
  3.1 4.1 %collective-permute-start = (f32[32,512]{1,0:T(8,128)S(1)}, f32[32,512]{1,0:T(8,128)S(1)}, u32[]{:S(2)}, u32[]{:S(2)}) collective-permute-start(f32[32,512]{1,0:T(8,128)S(1)} %get-tuple-element.8), channel_id=1, source_target_pairs={{0,4},{4,0},{8,12},{12,8},{1,5},{5,1},{9,13},{13,9},{2,6},{6,2},{1... | collective-permute-start | bytes 196616 | tf_op jit(solution)/shard_map/ppermute | solution.py:274
  4.1 12.4 %copy-start.2 = (bf16[2,256,256]{2,1,0:T(8,128)(2,1)S(1)}, bf16[2,256,256]{2,1,0:T(8,128)(2,1)}, u32[]{:S(2)}) copy-start(bf16[2,256,256]{2,1,0:T(8,128)(2,1)} %constant.7.clone.right_ref) | copy-start | bytes 786436
  4.1 12.4 %copy-start.3 = (bf16[128,432]{1,0:T(8,128)(2,1)S(1)}, bf16[128,432]{1,0:T(8,128)(2,1)}, u32[]{:S(2)}) copy-start(bf16[128,432]{1,0:T(8,128)(2,1)} %constant.8.clone.back_ref) | copy-start | bytes 331780
  4.1 6.0 %collective-permute-start.1 = (f32[32,512]{1,0:T(8,128)S(1)}, f32[32,512]{1,0:T(8,128)S(1)}, u32[]{:S(2)}, u32[]{:S(2)}) collective-permute-start(f32[32,512]{1,0:T(8,128)S(1)} %get-tuple-element.9), channel_id=1, source_target_pairs={{0,0},{4,8},{8,4},{12,12},{1,1},{5,9},{9,5},{13,13},{2,2},{6,10},{... | collective-permute-start | bytes 196616 | tf_op jit(solution)/shard_map/ppermute | solution.py:280
  10.3 6.1 %collective-permute-start.4 = (f32[144,128]{1,0:T(8,128)S(1)}, f32[144,128]{1,0:T(8,128)S(1)}, u32[]{:S(2)}, u32[]{:S(2)}) collective-permute-start(f32[144,128]{1,0:T(8,128)S(1)} %get-tuple-element.12), channel_id=1, source_target_pairs={{0,16},{16,0},{17,1},{1,17},{2,18},{18,2},{19,3},{3,19},{4,20},{20... | collective-permute-start | bytes 221192 | tf_op jit(solution)/shard_map/ppermute | solution.py:250
  10.6 4.7 %collective-permute-start.2 = (f32[80,128]{1,0:T(8,128)S(1)}, f32[80,128]{1,0:T(8,128)S(1)}, u32[]{:S(2)}, u32[]{:S(2)}) collective-permute-start(f32[80,128]{1,0:T(8,128)S(1)} %get-tuple-element.10), channel_id=1, source_target_pairs={{0,0},{16,17},{17,16},{1,2},{2,1},{18,19},{19,18},{3,3},{4,4},{20,... | collective-permute-start | bytes 122888 | tf_op jit(solution)/shard_map/ppermute | solution.py:250
  12.7 3.8 %collective-permute-start.5 = (f32[80,128]{1,0:T(8,128)S(1)}, f32[80,128]{1,0:T(8,128)S(1)}, u32[]{:S(2)}, u32[]{:S(2)}) collective-permute-start(f32[80,128]{1,0:T(8,128)S(1)} %get-tuple-element.13), channel_id=1, source_target_pairs={{0,17},{16,0},{17,2},{1,16},{2,19},{18,1},{19,3},{3,18},{4,21},{20... | collective-permute-start | bytes 122888 | tf_op jit(solution)/shard_map/ppermute | solution.py:250
  20.6 5.6 %collective-permute-start.8 = (f32[8,128]{1,0:T(8,128)S(1)}, f32[8,128]{1,0:T(8,128)S(1)}, u32[]{:S(2)}, u32[]{:S(2)}) collective-permute-start(f32[8,128]{1,0:T(8,128)S(1)} %shard_map.62.own_ref), channel_id=1, source_target_pairs={{0,16},{16,1},{17,0},{1,18},{2,17},{18,3},{19,2},{3,19},{4,20},{20... | collective-permute-start | bytes 12296 | tf_op jit(solution)/shard_map/ppermute | solution.py:250
  21.8 5.3 %collective-permute-start.7 = (f32[8,128]{1,0:T(8,128)S(1)}, f32[8,128]{1,0:T(8,128)S(1)}, u32[]{:S(2)}, u32[]{:S(2)}) collective-permute-start(f32[8,128]{1,0:T(8,128)S(1)} %shard_map.62.own_ref), channel_id=1, source_target_pairs={{0,0},{16,17},{17,16},{1,2},{2,1},{18,19},{19,18},{3,3},{4,4},{20,... | collective-permute-start | bytes 12296 | tf_op jit(solution)/shard_map/ppermute | solution.py:250
  26.1 2.5 %collective-permute-start.6 = (f32[8,128]{1,0:T(8,128)S(1)}, f32[8,128]{1,0:T(8,128)S(1)}, u32[]{:S(2)}, u32[]{:S(2)}) collective-permute-start(f32[8,128]{1,0:T(8,128)S(1)} %shard_map.62.own_ref), channel_id=1, source_target_pairs={{0,16},{16,0},{17,1},{1,17},{2,18},{18,2},{19,3},{3,19},{4,20},{20... | collective-permute-start | bytes 12296 | tf_op jit(solution)/shard_map/ppermute | solution.py:250
  28.7 7.4 %collective-permute-start.10 = (f32[8,128]{1,0:T(8,128)S(1)}, f32[8,128]{1,0:T(8,128)S(1)}, u32[]{:S(2)}, u32[]{:S(2)}) collective-permute-start(f32[8,128]{1,0:T(8,128)S(1)} %shard_map.63.own_ref), channel_id=1, source_target_pairs={{0,0},{4,8},{8,4},{12,12},{1,1},{5,9},{9,5},{13,13},{2,2},{6,10},{... | collective-permute-start | bytes 12296 | tf_op jit(solution)/shard_map/ppermute | solution.py:280
  34.8 1.3 %collective-permute-start.9 = (f32[8,128]{1,0:T(8,128)S(1)}, f32[8,128]{1,0:T(8,128)S(1)}, u32[]{:S(2)}, u32[]{:S(2)}) collective-permute-start(f32[8,128]{1,0:T(8,128)S(1)} %shard_map.63.own_ref), channel_id=1, source_target_pairs={{0,4},{4,0},{8,12},{12,8},{1,5},{5,1},{9,13},{13,9},{2,6},{6,2},{1... | collective-permute-start | bytes 12296 | tf_op jit(solution)/shard_map/ppermute | solution.py:274

commit v5 on v4

--- a/solution.py
+++ b/solution.py
@@ -58,15 +58,14 @@
 
 
 def node_order(cols):
-    return [2 * t for t in range(cols // 2)] + [2 * t + 1 for t in range(cols // 2)]
-
-
-def keep_region(region, wide, high_ref, low_ref):
-    even, odd = region[:, :wide], region[:, STRIDE:STRIDE + wide]
-    for part, values in enumerate((even, odd)):
-        high, low = split(values)
-        high_ref[:, part * wide:(part + 1) * wide] = high
-        low_ref[:, part * wide:(part + 1) * wide] = low
+    return [2 * t for t in range((cols + 1) // 2)] + [2 * t + 1 for t in range(cols // 2)]
+
+
+def keep_region(region, cols, high_ref, low_ref):
+    even = PATCH * ((cols + 1) // 2)
+    high_ref[:, :even], low_ref[:, :even] = split(region[:, :even])
+    if cols > 1:
+        high_ref[:, even:], low_ref[:, even:] = split(region[:, STRIDE:STRIDE + PATCH * (cols // 2)])
 
 
 def left_dft(cols, bands, high_ref, low_ref, left_ref, half_ref):
@@ -81,7 +80,7 @@
             half_ref[k * cols + j, :, PATCH:] = out[FREQ:, lanes]
 
 
-def correlate(rows, cols, group, sign, own_ref, other_ref, right_ref, back_ref, put,
+def correlate(rows, cols, group, sign, own_ref, other_ref, right_ref, back_ref, lane0, put,
               peak_ref, mass_ref, tilt_ref):
     row = lax.broadcasted_iota(jnp.int32, (group, FREQ, PATCH), 1)
     lane = lax.broadcasted_iota(jnp.int32, (group, FREQ, PATCH), 2)
@@ -115,7 +114,7 @@
     share = jnp.exp(peak - jnp.max(peak, axis=1, keepdims=True))
     mass = mass_ref[...] * share
     lag = lax.broadcasted_iota(jnp.int32, mass.shape, 1)
-    place = lax.broadcasted_iota(jnp.int32, mass.shape, 0) % cols
+    place = lax.broadcasted_iota(jnp.int32, mass.shape, 0) % cols + lane0
     here = lag == place
     lag = jnp.where(lag < PATCH // 2, lag, lag - PATCH).astype(jnp.float32)
     total = jnp.sum(mass, axis=1, keepdims=True)
@@ -130,17 +129,17 @@
 def flow_kernel(rows, cols, group, region_ref, left_ref, right_ref, back_ref, flow_ref,
                 high_ref, low_ref, own_ref, other_ref, *stats):
     for z, half_ref in enumerate((own_ref, other_ref)):
-        keep_region(region_ref[z], cols * STRIDE, high_ref, low_ref)
+        keep_region(region_ref[z], cols, high_ref, low_ref)
         left_dft(cols, range(rows), high_ref, low_ref, left_ref, half_ref)
 
     def put(c, i, row):
         flow_ref[c * rows + i:c * rows + i + 1, :] = row
 
-    correlate(rows, cols, group, 1.0, own_ref, other_ref, right_ref, back_ref, put, *stats)
+    correlate(rows, cols, group, 1.0, own_ref, other_ref, right_ref, back_ref, 0, put, *stats)
 
 
 def region_scratch(rows, cols):
-    return [pltpu.VMEM(((rows + 1) * STRIDE, 2 * cols * STRIDE), jnp.bfloat16)] * 2
+    return [pltpu.VMEM(((rows + 1) * STRIDE, cols * PATCH), jnp.bfloat16)] * 2
 
 
 def half_shape(rows, cols):
@@ -255,8 +254,7 @@
 
 
 def near(g, count):
-    to = g - 1 if g % 2 == 0 else g + 1
-    return to if 0 <= to < count else g
+    return (g - 1 if g % 2 == 0 else g + 1) % count
 
 
 def far(g, count):
@@ -276,8 +274,7 @@
 
 def pairs_odd(value):
     size = lax.axis_size("ty")
-    to = [i - 1 if i % 2 == 0 else i + 1 for i in range(size)]
-    return lax.ppermute(value, "ty", [(i, t if 0 <= t < size else i) for i, t in enumerate(to)])
+    return lax.ppermute(value, "ty", [(i, (i - 1 if i % 2 == 0 else i + 1) % size) for i in range(size)])
 
 
 def around(y, ny, even, odd):
@@ -301,16 +298,24 @@
     return jnp.concatenate([block[:, q * HALF:(q + 1) * HALF] for q in range(4)], axis=0)
 
 
-def packed_wide(value):
-    full = value.shape[1] // PATCH
-    tiles = [value[:, t * PATCH:(t + 1) * PATCH] for t in range(full)]
-    return jnp.concatenate(tiles + [packed(value[:, full * PATCH:])], axis=0)
-
-
-def unpacked_wide(block, tall, width):
-    full = width // PATCH
+def inner(half, value):
+    return value[:, HALF:] if half == 0 else value[:, :value.shape[1] - HALF]
+
+
+def outer(half, value):
+    return value[:, :HALF] if half == 0 else value[:, value.shape[1] - HALF:]
+
+
+def packed_wide(half, value):
+    tiles = inner(half, value)
+    blocks = [tiles[:, t * PATCH:(t + 1) * PATCH] for t in range(tiles.shape[1] // PATCH)]
+    return jnp.concatenate(blocks + [packed(outer(half, value))], axis=0)
+
+
+def unpacked_wide(block, tall):
+    full = block.shape[0] // tall
     tiles = [block[t * tall:(t + 1) * tall] for t in range(full)]
-    return jnp.concatenate(tiles + [unpacked(block[full * tall:full * tall + tall // 4])], axis=1)
+    return jnp.concatenate(tiles, axis=1), unpacked(block[full * tall:])
 
 
 def own_lanes(half, core, width):
@@ -331,7 +336,7 @@
     odd_ref[...] = jnp.where(lower, last, first)
 
     def branch(h):
-        other_ref[...] = packed_wide(tile_ref[:, own_lanes(1 - h, core, width)])
+        other_ref[...] = packed_wide(1 - h, tile_ref[:, own_lanes(1 - h, core, width)])
 
     by_half(half, branch)
 
@@ -348,51 +353,80 @@
 
     def branch(h):
         lanes = own_lanes(1 - h, core, width)
-        strips_ref[...] = packed_wide(jnp.concatenate([above[:, lanes], below[:, lanes]], axis=0))
+        strips_ref[...] = packed_wide(1 - h, jnp.concatenate([above[:, lanes], below[:, lanes]], axis=0))
         near_ref[...], past_ref[...] = (first, last) if h == 0 else (last, first)
 
     by_half(half, branch)
 
 
-def keep_half(half, x, nx, cols, side_ref, values, high_ref, low_ref):
+def border_patches(h, side, edge, tiles):
+    need = PATCH - 2 * HALF
+    if h == 0:
+        return jnp.concatenate([side, edge, tiles[:, :need]], axis=1)
+    return jnp.concatenate([tiles[:, tiles.shape[1] - need:], edge, side], axis=1)
+
+
+def masked_side(half, x, nx, side_ref):
     at_end = jnp.where(half == 0, x == 0, x == nx - 1)
-    side = jnp.where(at_end, 0.0, unpacked(side_ref[...]))
-
-    def branch(h):
-        value = jnp.concatenate([side, values(h)] if h == 0 else [values(h), side], axis=1)
-        keep_region(value, cols * STRIDE, high_ref, low_ref)
-
-    by_half(half, branch)
-
-
-def own_kernel(rows, cols, ny, nx, tile_ref, even_ref, odd_ref, side_ref, left_ref, half_ref, high_ref, low_ref):
+    return jnp.where(at_end, 0.0, unpacked(side_ref[...]))
+
+
+def own_kernel(rows, cols, ny, nx, tile_ref, even_ref, odd_ref, side_ref, left_ref, free_ref, border_ref,
+               high_ref, low_ref, border_high, border_low):
     _, y, x, half = where_am_i()
     width, core = tile_ref.shape[1], cols * STRIDE + HALF
     above, below = around(y, ny, even_ref[...], odd_ref[...])
-
-    def values(h):
+    side = masked_side(half, x, nx, side_ref)
+
+    def branch(h):
         lanes = own_lanes(h, core, width)
-        return jnp.concatenate([above[:, lanes], tile_ref[:, lanes], below[:, lanes]], axis=0)
-
-    keep_half(half, x, nx, cols, side_ref, values, high_ref, low_ref)
-    left_dft(cols, range(rows), high_ref, low_ref, left_ref, half_ref)
-
-
-def pair_kernel(rows, cols, group, nx, own_ref, other_ref, strips_ref, cross_ref,
-                left_ref, right_ref, back_ref, flow_ref, high_ref, low_ref, half_ref, *stats):
-    section, _, x, half = where_am_i()
-    core = cols * STRIDE + HALF
-    strips = unpacked_wide(strips_ref[...], 2 * HALF, core)
-    middle = unpacked_wide(other_ref[...], rows * STRIDE, core)
-    value = jnp.concatenate([strips[:HALF], middle, strips[HALF:]], axis=0)
-    keep_half(half, x, nx, cols, cross_ref, lambda h: value, high_ref, low_ref)
-    left_dft(cols, range(rows), high_ref, low_ref, left_ref, half_ref)
+        value = jnp.concatenate([above[:, lanes], tile_ref[:, lanes], below[:, lanes]], axis=0)
+        tiles = inner(h, value)
+        keep_region(tiles, cols - 1, high_ref, low_ref)
+        keep_region(border_patches(h, side, outer(h, value), tiles), 1, border_high, border_low)
+
+    by_half(half, branch)
+    left_dft(cols - 1, range(rows), high_ref, low_ref, left_ref, free_ref)
+    left_dft(1, range(rows), border_high, border_low, left_ref, border_ref)
+
+
+def other_parts(rows, other_ref, strips_ref):
+    tiles, edge = unpacked_wide(other_ref[...], rows * STRIDE)
+    more_tiles, more_edge = unpacked_wide(strips_ref[...], 2 * HALF)
+    return (jnp.concatenate([more[:HALF], middle, more[HALF:]], axis=0)
+            for more, middle in ((more_tiles, tiles), (more_edge, edge)))
+
+
+def free_kernel(rows, cols, own_ref, other_ref, strips_ref, left_ref, right_ref, back_ref, flow_ref,
+                high_ref, low_ref, half_ref, *stats):
+    section, _, _, half = where_am_i()
+    tiles, _ = other_parts(rows, other_ref, strips_ref)
+    keep_region(tiles, cols - 1, high_ref, low_ref)
+    left_dft(cols - 1, range(rows), high_ref, low_ref, left_ref, half_ref)
 
     def put(c, i, row):
         flow_ref[c * rows + i:c * rows + i + 1, :] = row
 
     sign = jnp.where(section == 0, 1.0, -1.0)
-    correlate(rows, cols, group, sign, own_ref, half_ref, right_ref, back_ref, put, *stats)
+    count = rows * (cols - 1)
+    correlate(rows, cols - 1, count, sign, own_ref, half_ref, right_ref, back_ref, 1 - half, put, *stats)
+
+
+def border_kernel(rows, cols, nx, own_ref, other_ref, strips_ref, cross_ref, before_ref, left_ref, right_ref,
+                  back_ref, flow_ref, high_ref, low_ref, half_ref, *stats):
+    section, _, x, half = where_am_i()
+    tiles, edge = other_parts(rows, other_ref, strips_ref)
+    side = masked_side(half, x, nx, cross_ref)
+    by_half(half, lambda h: keep_region(border_patches(h, side, edge, tiles), 1, high_ref, low_ref))
+    left_dft(1, range(rows), high_ref, low_ref, left_ref, half_ref)
+
+    def put(c, i, row):
+        at = slice(c * rows + i, c * rows + i + 1)
+        flow_ref[at, :] = before_ref[at, :] + row
+
+    sign = jnp.where(section == 0, 1.0, -1.0)
+    lane = (cols - 1) * half
+    correlate(rows, 1, rows, sign, own_ref, half_ref, right_ref, back_ref, lane, put, *stats)
 
 
 def window_kernel(width, nx, own_ref, mate_ref, near_ref, far_ref, out_ref):
@@ -461,15 +495,21 @@
     side, cross = along(side, near), along(cross, past)
     strips = along(strips, mate)
     left, right, back = tables()
-    spectra = half_shape(rows, half)
-    own = kernel_call(
-        functools.partial(own_kernel, rows, half, ny, nx), floats(*spectra), tile, even, odd, side, left,
-        scratch=region_scratch(rows, half),
+    free, border = half_shape(rows, half - 1), half_shape(rows, 1)
+    own_free, own_border = kernel_call(
+        functools.partial(own_kernel, rows, half, ny, nx), (floats(*free), floats(*border)),
+        tile, even, odd, side, left,
+        scratch=region_scratch(rows, half - 1) + region_scratch(rows, 1),
     )
     flow = kernel_call(
-        functools.partial(pair_kernel, rows, half, rows * half, nx), floats(2 * rows, PATCH),
-        own, other, strips, cross, left, right, back,
-        scratch=region_scratch(rows, half) + [pltpu.VMEM(spectra, jnp.float32)] + stats_scratch(rows, half),
+        functools.partial(free_kernel, rows, half), floats(2 * rows, PATCH),
+        own_free, other, strips, left, right, back,
+        scratch=region_scratch(rows, half - 1) + [pltpu.VMEM(free, jnp.float32)] + stats_scratch(rows, half - 1),
+    )
+    flow = kernel_call(
+        functools.partial(border_kernel, rows, half, nx), floats(2 * rows, PATCH),
+        own_border, other, strips, cross, flow, left, right, back,
+        scratch=region_scratch(rows, 1) + [pltpu.VMEM(border, jnp.float32)] + stats_scratch(rows, 1),
     )
     window = kernel_call(
         functools.partial(window_kernel, half, nx), floats(*flow.shape),

time: 37.2 us -> 33.1 us (0.89)
  the two profiles are of different devices: /device:TPU:17 before, /device:TPU:0 now
where the time goes in v5:
time: 33.1 us; the launch traced here: 32.9 us
  starting transfers between devices  14.4 us (44%)
  waiting for transfers between devices  9.55 us (29%)
  Pallas kernels  7.19 us (22%)
  local copies, waits for them, and re-layouts  1.05 us (3%)
  between operations  0.73 us (2%)
    ppermute x7, starting transfers between devices, along(): return lax.ppermute(value, AXES, pairs)  11.2 us
    pallas_call x7, Pallas kernels, kernel_call(): pl.pallas_call(body, out_shape=shapes, in_specs=[IN_VMEM] * len(args), ou...  7.19 us
    ppermute x7, waiting for transfers between devices, along(): return lax.ppermute(value, AXES, pairs)  6.02 us
    ppermute x2, waiting for transfers between devices, pairs_odd(): lax.ppermute(value, 'ty', [(i, (i - 1 if i % 2 == 0 else i + 1) % size) f...  3.52 us
    ppermute x2, starting transfers between devices, pairs_odd(): lax.ppermute(value, 'ty', [(i, (i - 1 if i % 2 == 0 else i + 1) % size) f...  1.61 us
    ppermute x2, starting transfers between devices, pairs_even(): return lax.ppermute(value, 'ty', [(i, i ^ 1) for i in range(size)])  1.59 us
    unnamed x8, local copies, waits for them, and re-layouts  1.05 us
  transfers between devices with their start and end apart: 11, of which 6 were waited for; matrix products, arithmetic and copies ran while one was open for 0% of the time, Pallas kernels for 13%

profile of v5, /device:TPU:0, one launch (start us, length us, event | category | flops | bytes accessed | tf_op | source)
XLA Modules:
  0.0 32.9 jit_solution(11075869076782508879)
XLA Ops:
  0.6 0.0 copy-start
  0.6 1.0 %copy-done = f32[1,256,512]{2,1,0:T(8,128)S(1)} copy-done((f32[1,256,512]{2,1,0:T(8,128)S(1)}, f32[1,256,512]{2,1,0:T(8,128)}, u32[]{:S(2)}) %copy-start) | copy-done | bytes 524312
  1.7 0.2 shard_map.59
  1.9 3.1 %collective-permute-start.3 = (f32[576,128]{1,0:T(8,128)S(1)}, f32[576,128]{1,0:T(8,128)S(1)}, u32[]{:S(2)}, u32[]{:S(2)}) collective-permute-start(f32[576,128]{1,0:T(8,128)S(1)} %get-tuple-element.14), channel_id=1, source_target_pairs={{0,16},{16,0},{17,1},{1,17},{2,18},{18,2},{19,3},{3,19},{4,20},{20... | collective-permute-start | bytes 884744 | tf_op jit(solution)/shard_map/ppermute | solution.py:249
  5.0 0.0 collective-permute-start
  5.0 0.0 copy-start.2
  5.0 1.6 %collective-permute-start.1 = (f32[32,512]{1,0:T(8,128)S(1)}, f32[32,512]{1,0:T(8,128)S(1)}, u32[]{:S(2)}, u32[]{:S(2)}) collective-permute-start(f32[32,512]{1,0:T(8,128)S(1)} %get-tuple-element.11), channel_id=1, source_target_pairs={{0,12},{4,8},{8,4},{12,0},{1,13},{5,9},{9,5},{13,1},{2,14},{6,10},... | collective-permute-start | bytes 196616 | tf_op jit(solution)/shard_map/ppermute | solution.py:277
  6.6 0.0 collective-permute-done.even_ref
  6.6 2.1 %collective-permute-done.1.odd_ref = f32[32,512]{1,0:T(8,128)S(1)} collective-permute-done((f32[32,512]{1,0:T(8,128)S(1)}, f32[32,512]{1,0:T(8,128)S(1)}, u32[]{:S(2)}, u32[]{:S(2)}) %collective-permute-start.1) | collective-permute-done | bytes 65568 | tf_op jit(solution)/shard_map/ppermute | solution.py:277
  8.7 0.3 shard_map.60
  8.9 0.8 %collective-permute-start.4 = (f32[144,128]{1,0:T(8,128)S(1)}, f32[144,128]{1,0:T(8,128)S(1)}, u32[]{:S(2)}, u32[]{:S(2)}) collective-permute-start(f32[144,128]{1,0:T(8,128)S(1)} %get-tuple-element.15), channel_id=1, source_target_pairs={{0,16},{16,0},{17,1},{1,17},{2,18},{18,2},{19,3},{3,19},{4,20},{20... | collective-permute-start | bytes 221192 | tf_op jit(solution)/shard_map/ppermute | solution.py:249
  9.7 3.4 %collective-permute-start.2 = (f32[80,128]{1,0:T(8,128)S(1)}, f32[80,128]{1,0:T(8,128)S(1)}, u32[]{:S(2)}, u32[]{:S(2)}) collective-permute-start(f32[80,128]{1,0:T(8,128)S(1)} %get-tuple-element.12), channel_id=1, source_target_pairs={{0,3},{16,17},{17,16},{1,2},{2,1},{18,19},{19,18},{3,0},{4,7},{20,... | collective-permute-start | bytes 122888 | tf_op jit(solution)/shard_map/ppermute | solution.py:249
  13.1 0.0 copy-start.1
  13.1 0.0 copy-start.3
  13.1 0.0 collective-permute-start.5
  13.1 2.4 %collective-permute-done.2.side_ref = f32[80,128]{1,0:T(8,128)S(1)} collective-permute-done((f32[80,128]{1,0:T(8,128)S(1)}, f32[80,128]{1,0:T(8,128)S(1)}, u32[]{:S(2)}, u32[]{:S(2)}) %collective-permute-start.2) | collective-permute-done | bytes 40992 | tf_op jit(solution)/shard_map/ppermute | solution.py:249
  15.5 0.0 copy-done.2
  15.5 1.1 %shard_map.61 = (f32[12,72,256]{2,1,0:T(8,128)S(1)}, f32[4,72,256]{2,1,0:T(8,128)S(1)}) custom-call(f32[256,512]{1,0:T(8,128)S(1)} %bitcast.3, f32[32,512]{1,0:T(8,128)S(1)} %collective-permute-done.even_ref, f32[32,512]{1,0:T(8,128)S(1)} %collective-permute-done.1.odd_ref, f32[80,128]{1,0:T(8,128)S(1)} %collective-permute-done.2.side_ref, ...), custom_call_target="tpu_custom_call" | custom-call | tf_op jit(solution)/shard_map/pallas_call | solution.py:159
  16.6 0.0 collective-permute-done.4.strips_ref
  16.6 0.0 collective-permute-done.3.other_ref
  16.6 0.0 copy-done.1
  16.6 0.0 copy-done.3
  16.6 3.0 %shard_map.62.before_ref = f32[8,128]{1,0:T(8,128)S(1)} custom-call(f32[12,72,256]{2,1,0:T(8,128)S(1)} %get-tuple-element.17.own_ref, f32[576,128]{1,0:T(8,128)S(1)} %collective-permute-done.3.other_ref, f32[144,128]{1,0:T(8,128)S(1)} %collective-permute-done.4.strips_ref, bf16[144,384]{1,0:T(8,128)(2,1)S(1)} %copy-done.2, ...), custom_call_target="tpu_custom_call" | custom-call | tf_op jit(solution)/shard_map/pallas_call | solution.py:159
  19.7 0.0 collective-permute-done.5.cross_ref
  19.7 1.7 %shard_map.63.own_ref = f32[8,128]{1,0:T(8,128)S(1)} custom-call(f32[4,72,256]{2,1,0:T(8,128)S(1)} %get-tuple-element.13.own_ref, f32[576,128]{1,0:T(8,128)S(1)} %collective-permute-done.3.other_ref, f32[144,128]{1,0:T(8,128)S(1)} %collective-permute-done.4.strips_ref, f32[80,128]{1,0:T(8,128)S(1)} %collective-permute-done.5.cross_ref, ...), custom_call_target="tpu_custom_call" | custom-call | tf_op jit(solution)/shard_map/pallas_call | solution.py:159
  21.4 0.0 collective-permute-start.8
  21.4 4.0 %collective-permute-start.7 = (f32[8,128]{1,0:T(8,128)S(1)}, f32[8,128]{1,0:T(8,128)S(1)}, u32[]{:S(2)}, u32[]{:S(2)}) collective-permute-start(f32[8,128]{1,0:T(8,128)S(1)} %shard_map.63.own_ref), channel_id=1, source_target_pairs={{0,3},{16,17},{17,16},{1,2},{2,1},{18,19},{19,18},{3,0},{4,7},{20,... | collective-permute-start | bytes 12296 | tf_op jit(solution)/shard_map/ppermute | solution.py:249
  25.4 0.0 collective-permute-start.6
  25.4 0.5 %collective-permute-done.8.far_ref = f32[8,128]{1,0:T(8,128)S(1)} collective-permute-done((f32[8,128]{1,0:T(8,128)S(1)}, f32[8,128]{1,0:T(8,128)S(1)}, u32[]{:S(2)}, u32[]{:S(2)}) %collective-permute-start.8) | collective-permute-done | bytes 4128 | tf_op jit(solution)/shard_map/ppermute | solution.py:249
  25.9 1.1 %collective-permute-done.7.near_ref = f32[8,128]{1,0:T(8,128)S(1)} collective-permute-done((f32[8,128]{1,0:T(8,128)S(1)}, f32[8,128]{1,0:T(8,128)S(1)}, u32[]{:S(2)}, u32[]{:S(2)}) %collective-permute-start.7) | collective-permute-done | bytes 4128 | tf_op jit(solution)/shard_map/ppermute | solution.py:249
  27.0 2.0 %collective-permute-done.6.mate_ref = f32[8,128]{1,0:T(8,128)S(1)} collective-permute-done((f32[8,128]{1,0:T(8,128)S(1)}, f32[8,128]{1,0:T(8,128)S(1)}, u32[]{:S(2)}, u32[]{:S(2)}) %collective-permute-start.6) | collective-permute-done | bytes 4128 | tf_op jit(solution)/shard_map/ppermute | solution.py:249
  29.0 0.1 shard_map.64.own_ref
  29.1 0.0 collective-permute-start.10
  29.1 1.6 %collective-permute-start.9 = (f32[8,128]{1,0:T(8,128)S(1)}, f32[8,128]{1,0:T(8,128)S(1)}, u32[]{:S(2)}, u32[]{:S(2)}) collective-permute-start(f32[8,128]{1,0:T(8,128)S(1)} %shard_map.64.own_ref), channel_id=1, source_target_pairs={{0,4},{4,0},{8,12},{12,8},{1,5},{5,1},{9,13},{13,9},{2,6},{6,2},{1... | collective-permute-start | bytes 12296 | tf_op jit(solution)/shard_map/ppermute | solution.py:272
  30.7 1.4 %collective-permute-done.10.odd_ref = f32[8,128]{1,0:T(8,128)S(1)} collective-permute-done((f32[8,128]{1,0:T(8,128)S(1)}, f32[8,128]{1,0:T(8,128)S(1)}, u32[]{:S(2)}, u32[]{:S(2)}) %collective-permute-start.10) | collective-permute-done | bytes 4128 | tf_op jit(solution)/shard_map/ppermute | solution.py:277
  32.1 0.0 collective-permute-done.9.even_ref
  32.1 0.8 %shard_map.65 = (f32[1,2,4,8]{3,2,1,0:T(4,128)}, f32[1,2,4,8]{3,2,1,0:T(4,128)}) custom-call(f32[8,128]{1,0:T(8,128)S(1)} %shard_map.64.own_ref, f32[8,128]{1,0:T(8,128)S(1)} %collective-permute-done.9.even_ref, f32[8,128]{1,0:T(8,128)S(1)} %collective-permute-done.10.odd_ref), custom_call_target="tpu_custom_call" | custom-call | tf_op jit(solution)/shard_map/pallas_call | solution.py:159
Async XLA Ops:
  0.6 1.0 %copy-start = (f32[1,256,512]{2,1,0:T(8,128)S(1)}, f32[1,256,512]{2,1,0:T(8,128)}, u32[]{:S(2)}) copy-start(f32[1,256,512]{2,1,0:T(8,128)} %param.4) | copy-start | bytes 1572868
  1.9 14.7 %collective-permute-start.3 = (f32[576,128]{1,0:T(8,128)S(1)}, f32[576,128]{1,0:T(8,128)S(1)}, u32[]{:S(2)}, u32[]{:S(2)}) collective-permute-start(f32[576,128]{1,0:T(8,128)S(1)} %get-tuple-element.14), channel_id=1, source_target_pairs={{0,16},{16,0},{17,1},{1,17},{2,18},{18,2},{19,3},{3,19},{4,20},{20... | collective-permute-start | bytes 884744 | tf_op jit(solution)/shard_map/ppermute | solution.py:249
  5.0 1.6 %collective-permute-start = (f32[32,512]{1,0:T(8,128)S(1)}, f32[32,512]{1,0:T(8,128)S(1)}, u32[]{:S(2)}, u32[]{:S(2)}) collective-permute-start(f32[32,512]{1,0:T(8,128)S(1)} %get-tuple-element.10), channel_id=1, source_target_pairs={{0,4},{4,0},{8,12},{12,8},{1,5},{5,1},{9,13},{13,9},{2,6},{6,2},{1... | collective-permute-start | bytes 196616 | tf_op jit(solution)/shard_map/ppermute | solution.py:272
  5.0 10.5 %copy-start.2 = (bf16[144,384]{1,0:T(8,128)(2,1)S(1)}, bf16[144,384]{1,0:T(8,128)(2,1)}, u32[]{:S(2)}) copy-start(bf16[144,384]{1,0:T(8,128)(2,1)} %constant.6.clone.left_ref) | copy-start | bytes 331780
  5.0 3.7 %collective-permute-start.1 = (f32[32,512]{1,0:T(8,128)S(1)}, f32[32,512]{1,0:T(8,128)S(1)}, u32[]{:S(2)}, u32[]{:S(2)}) collective-permute-start(f32[32,512]{1,0:T(8,128)S(1)} %get-tuple-element.11), channel_id=1, source_target_pairs={{0,12},{4,8},{8,4},{12,0},{1,13},{5,9},{9,5},{13,1},{2,14},{6,10},... | collective-permute-start | bytes 196616 | tf_op jit(solution)/shard_map/ppermute | solution.py:277
  8.9 7.7 %collective-permute-start.4 = (f32[144,128]{1,0:T(8,128)S(1)}, f32[144,128]{1,0:T(8,128)S(1)}, u32[]{:S(2)}, u32[]{:S(2)}) collective-permute-start(f32[144,128]{1,0:T(8,128)S(1)} %get-tuple-element.15), channel_id=1, source_target_pairs={{0,16},{16,0},{17,1},{1,17},{2,18},{18,2},{19,3},{3,19},{4,20},{20... | collective-permute-start | bytes 221192 | tf_op jit(solution)/shard_map/ppermute | solution.py:249
  9.7 5.8 %collective-permute-start.2 = (f32[80,128]{1,0:T(8,128)S(1)}, f32[80,128]{1,0:T(8,128)S(1)}, u32[]{:S(2)}, u32[]{:S(2)}) collective-permute-start(f32[80,128]{1,0:T(8,128)S(1)} %get-tuple-element.12), channel_id=1, source_target_pairs={{0,3},{16,17},{17,16},{1,2},{2,1},{18,19},{19,18},{3,0},{4,7},{20,... | collective-permute-start | bytes 122888 | tf_op jit(solution)/shard_map/ppermute | solution.py:249
  13.1 3.5 %copy-start.1 = (bf16[2,256,256]{2,1,0:T(8,128)(2,1)S(1)}, bf16[2,256,256]{2,1,0:T(8,128)(2,1)}, u32[]{:S(2)}) copy-start(bf16[2,256,256]{2,1,0:T(8,128)(2,1)} %constant.7.clone.right_ref) | copy-start | bytes 786436
  13.1 3.5 %copy-start.3 = (bf16[128,432]{1,0:T(8,128)(2,1)S(1)}, bf16[128,432]{1,0:T(8,128)(2,1)}, u32[]{:S(2)}) copy-start(bf16[128,432]{1,0:T(8,128)(2,1)} %constant.8.clone.back_ref) | copy-start | bytes 331780
  13.1 6.6 %collective-permute-start.5 = (f32[80,128]{1,0:T(8,128)S(1)}, f32[80,128]{1,0:T(8,128)S(1)}, u32[]{:S(2)}, u32[]{:S(2)}) collective-permute-start(f32[80,128]{1,0:T(8,128)S(1)} %get-tuple-element.16), channel_id=1, source_target_pairs={{0,17},{16,0},{17,2},{1,16},{2,19},{18,1},{19,3},{3,18},{4,21},{20... | collective-permute-start | bytes 122888 | tf_op jit(solution)/shard_map/ppermute | solution.py:249
  21.4 4.5 %collective-permute-start.8 = (f32[8,128]{1,0:T(8,128)S(1)}, f32[8,128]{1,0:T(8,128)S(1)}, u32[]{:S(2)}, u32[]{:S(2)}) collective-permute-start(f32[8,128]{1,0:T(8,128)S(1)} %shard_map.63.own_ref), channel_id=1, source_target_pairs={{0,16},{16,1},{17,0},{1,18},{2,17},{18,3},{19,2},{3,19},{4,20},{20... | collective-permute-start | bytes 12296 | tf_op jit(solution)/shard_map/ppermute | solution.py:249
  21.4 5.6 %collective-permute-start.7 = (f32[8,128]{1,0:T(8,128)S(1)}, f32[8,128]{1,0:T(8,128)S(1)}, u32[]{:S(2)}, u32[]{:S(2)}) collective-permute-start(f32[8,128]{1,0:T(8,128)S(1)} %shard_map.63.own_ref), channel_id=1, source_target_pairs={{0,3},{16,17},{17,16},{1,2},{2,1},{18,19},{19,18},{3,0},{4,7},{20,... | collective-permute-start | bytes 12296 | tf_op jit(solution)/shard_map/ppermute | solution.py:249
  25.4 3.6 %collective-permute-start.6 = (f32[8,128]{1,0:T(8,128)S(1)}, f32[8,128]{1,0:T(8,128)S(1)}, u32[]{:S(2)}, u32[]{:S(2)}) collective-permute-start(f32[8,128]{1,0:T(8,128)S(1)} %shard_map.63.own_ref), channel_id=1, source_target_pairs={{0,16},{16,0},{17,1},{1,17},{2,18},{18,2},{19,3},{3,19},{4,20},{20... | collective-permute-start | bytes 12296 | tf_op jit(solution)/shard_map/ppermute | solution.py:249
  29.1 3.0 %collective-permute-start.10 = (f32[8,128]{1,0:T(8,128)S(1)}, f32[8,128]{1,0:T(8,128)S(1)}, u32[]{:S(2)}, u32[]{:S(2)}) collective-permute-start(f32[8,128]{1,0:T(8,128)S(1)} %shard_map.64.own_ref), channel_id=1, source_target_pairs={{0,12},{4,8},{8,4},{12,0},{1,13},{5,9},{9,5},{13,1},{2,14},{6,10},... | collective-permute-start | bytes 12296 | tf_op jit(solution)/shard_map/ppermute | solution.py:277
  29.1 3.0 %collective-permute-start.9 = (f32[8,128]{1,0:T(8,128)S(1)}, f32[8,128]{1,0:T(8,128)S(1)}, u32[]{:S(2)}, u32[]{:S(2)}) collective-permute-start(f32[8,128]{1,0:T(8,128)S(1)} %shard_map.64.own_ref), channel_id=1, source_target_pairs={{0,4},{4,0},{8,12},{12,8},{1,5},{5,1},{9,13},{13,9},{2,6},{6,2},{1... | collective-permute-start | bytes 12296 | tf_op jit(solution)/shard_map/ppermute | solution.py:272
